TPU v7x, 32 devices: a whole 2x2x4 slice. The times are simulated.
32 devices in a mesh: mem: 4 (over z), lat: 8 (over y, x, core).
Axes of the slice: x: 2, y: 2, z: 4, core: 2. Of those that a mesh axis runs over, the one named last changes fastest.
Arguments:
- features: bfloat16 [16, 16, 1440, 128], P('mem', 'lat'), may hold values from -6 to 6
- conv_inner: bfloat16 [3, 3, 128, 128], replicated, may hold values from -0.1875 to 0.1875
- conv_head: bfloat16 [3, 3, 128, 69], replicated, may hold values from -0.1875 to 0.1875
- truth: float32 [69, 16, 1440], P(None, 'lat'), may hold values from -5 to 5
- kernel_width: float32 [69], replicated, may hold values from 0.3 to 1.5
- var_weight: float32 [69], replicated, may hold values from 0.5 to 2
Outputs:
- grad_features: bfloat16 [16, 16, 1440, 128], P('mem', 'lat')
- grad_inner: float32 [3, 3, 128, 128], replicated
- grad_head: float32 [3, 3, 128, 69], replicated
All inputs are finite; a program needn't handle non-finite values.
Results may differ from a plain program's by a relative error of at most 0.0098.
Values may be sent and summed in bfloat16 or wider, within the bound.
No kernel may reach another device: no remote copies, remote signals or barrier semaphores. Data moves between devices by JAX's collectives and lax.ppermute only.
A program may use at most 256 MiB of HBM per device.

v0:
```python
import jax
import jax.numpy as jnp
from jax import lax
from jax.sharding import PartitionSpec as P


def padded_2(cells, sides, width):
    for axis, dim in sides:
        count = lax.axis_size(axis)
        ends = count - 1
        head = lax.slice_in_dim(cells, 0, width, axis=dim)
        tail = lax.slice_in_dim(cells, cells.shape[dim] - width, cells.shape[dim], axis=dim)
        cells = jnp.concatenate(
            [
                lax.ppermute(tail, axis, [(i, (i + 1) % count) for i in range(ends)]),
                cells,
                lax.ppermute(head, axis, [((i + 1) % count, i) for i in range(ends)]),
            ],
            axis=dim,
        )
    return cells


def wrap_lon(values, axis):
    count = values.shape[axis]
    return jnp.concatenate(
        [
            lax.slice_in_dim(values, count - 1, count, axis=axis),
            values,
            lax.slice_in_dim(values, 0, 1, axis=axis),
        ],
        axis=axis,
    )


def gelu_slope(pre):
    return jax.jvp(jax.nn.gelu, (pre,), (jnp.ones_like(pre),))[1]


def hidden_conv(padded, kernel, band_rows):
    lon_cells = padded.shape[2] - 2
    summed = jnp.zeros((padded.shape[0], band_rows, lon_cells, kernel.shape[3]), jnp.float32)
    for row_off in range(3):
        for col_off in range(3):
            summed = summed + jnp.einsum(
                "mrlc,co->mrlo",
                padded[:, row_off : row_off + band_rows, col_off : col_off + lon_cells],
                kernel[row_off, col_off],
                preferred_element_type=jnp.float32,
            )
    return summed


def field_conv(padded, kernel, band_rows):
    lon_cells = padded.shape[2] - 2
    summed = jnp.zeros((padded.shape[0], kernel.shape[3], band_rows, lon_cells), jnp.float32)
    for row_off in range(3):
        for col_off in range(3):
            summed = summed + jnp.einsum(
                "mrlc,cv->mvrl",
                padded[:, row_off : row_off + band_rows, col_off : col_off + lon_cells],
                kernel[row_off, col_off],
                preferred_element_type=jnp.float32,
            )
    return summed


def field_back(padded_grad, kernel, band_rows):
    lon_cells = padded_grad.shape[3] - 2
    summed = jnp.zeros((padded_grad.shape[0], band_rows, lon_cells, kernel.shape[2]), jnp.float32)
    for row_off in range(3):
        for col_off in range(3):
            summed = summed + jnp.einsum(
                "mvrl,cv->mrlc",
                padded_grad[
                    :,
                    :,
                    2 - row_off : 2 - row_off + band_rows,
                    2 - col_off : 2 - col_off + lon_cells,
                ],
                kernel[row_off, col_off],
                preferred_element_type=jnp.float32,
            )
    return summed


def hidden_back(padded_grad, kernel, band_rows):
    lon_cells = padded_grad.shape[2] - 2
    summed = jnp.zeros((padded_grad.shape[0], band_rows, lon_cells, kernel.shape[2]), jnp.float32)
    for row_off in range(3):
        for col_off in range(3):
            summed = summed + jnp.einsum(
                "mrlo,co->mrlc",
                padded_grad[
                    :, 2 - row_off : 2 - row_off + band_rows, 2 - col_off : 2 - col_off + lon_cells
                ],
                kernel[row_off, col_off],
                preferred_element_type=jnp.float32,
            )
    return summed


def kernel_grad(padded_input, grad_out, form, band_rows, lon_cells):
    pieces = []
    for row_off in range(3):
        for col_off in range(3):
            pieces.append(
                jnp.einsum(
                    form,
                    padded_input[:, row_off : row_off + band_rows, col_off : col_off + lon_cells],
                    grad_out,
                    preferred_element_type=jnp.float32,
                )
            )
    return jnp.stack(pieces).reshape((3, 3) + pieces[0].shape)


def pair_sums(own, others, inverse):
    spread = others[None] - own[:, None]
    kernel = jnp.exp(-0.5 * spread * spread * inverse[None, None, :, None, None])
    return jnp.sum(kernel * spread, axis=1)


def member_grad(own, pairwise, truth_piece, inverse, var_weight, members):
    offset = own - truth_piece[None]
    nearness = jnp.exp(-0.5 * offset * offset * inverse[None, :, None, None])
    scale = (var_weight * inverse)[None, :, None, None]
    return scale * (2.0 / (members - 1) * pairwise + 2.0 * nearness * offset)


def split_groups(values, blocks, group):
    shaped = values.reshape((values.shape[0], blocks, group) + values.shape[2:])
    return jnp.moveaxis(shaped, 1, 0)


def shards(features, conv_inner, conv_head, truth, kernel_width, var_weight):
    band_rows = features.shape[1]
    lon_cells = features.shape[2]
    variables = conv_head.shape[3]
    feature_ext = padded_2(features, (("lat", 1),), 1)
    pre_own = hidden_conv(wrap_lon(feature_ext, 2), conv_inner, band_rows)
    hidden_own = jax.nn.gelu(pre_own).astype(jnp.bfloat16)
    hidden_ext = padded_2(hidden_own, (("lat", 1),), 1)
    hidden_wrap = wrap_lon(hidden_ext, 2)
    field = field_conv(hidden_wrap, conv_head, band_rows).astype(jnp.bfloat16)
    inverse = 1.0 / (kernel_width * kernel_width)
    group = 3
    blocks = variables // group
    inverse_blocks = inverse.reshape(blocks, group)
    gathered = lax.all_to_all(field, "mem", split_axis=3, concat_axis=0, tiled=True)
    values = gathered.astype(jnp.float32)
    members = values.shape[0]
    piece_cells = values.shape[3]

    def block_pairs(packed):
        member_values, rates = packed
        return pair_sums(member_values, member_values, rates)

    pairwise = lax.map(block_pairs, (split_groups(values, blocks, group), inverse_blocks))
    pairwise = jnp.moveaxis(pairwise, 0, 1).reshape(values.shape)
    truth_piece = lax.dynamic_slice_in_dim(
        truth, lax.axis_index("mem") * piece_cells, piece_cells, 2
    )
    gradient = member_grad(values, pairwise, truth_piece, inverse, var_weight, members).astype(
        jnp.bfloat16
    )
    field_grad = lax.all_to_all(gradient, "mem", split_axis=0, concat_axis=3, tiled=True)
    grad_pad = padded_2(field_grad, (("lat", 2),), 1)
    hidden_grad = (
        field_back(wrap_lon(grad_pad, 3), conv_head, band_rows) * gelu_slope(pre_own)
    ).astype(jnp.bfloat16)
    head_grad = kernel_grad(hidden_wrap, field_grad, "mrlc,mvrl->cv", band_rows, lon_cells)
    hidden_pad = padded_2(hidden_grad, (("lat", 1),), 1)
    grad_features = hidden_back(wrap_lon(hidden_pad, 2), conv_inner, band_rows).astype(jnp.bfloat16)
    inner_grad = kernel_grad(
        wrap_lon(feature_ext, 2), hidden_grad, "mrlc,mrlo->co", band_rows, lon_cells
    )
    inner_sum, head_sum = lax.psum((inner_grad, head_grad), ("mem", "lat"))
    points = band_rows * lax.axis_size("lat") * lon_cells
    return (grad_features, inner_sum / points, head_sum / points)


def solution(mesh):
    in_specs = (P("mem", "lat", None, None), P(), P(), P(None, "lat", None), P(), P())
    out_specs = (P("mem", "lat", None, None), P(), P())
    return jax.shard_map(shards, mesh=mesh, in_specs=in_specs, out_specs=out_specs, check_vma=False)
```

profile of v0, /device:TPU:0, one launch (start us, length us, event | category | flops | bytes accessed | tf_op | source)
XLA Modules:
  0.0 686.2 jit_solution(3638382335253527599)
XLA Ops:
  19.7 4.1 fusion.183
  23.7 4.0 fusion.173
  44.7 21.2 %multiply_convert_fusion = (bf16[4,2,1440,128]{3,2,1,0:T(8,128)(2,1)}, f32[4,2,1440,128]{3,2,1,0:T(8,128)}) fusion(bf16[3,3,128,128]{3,2,1,0:T(8,128)(2,1)S(1)} %copy-done.21, bf16[4,4,1,128]{3,2,1,0:T(2,128)(2,1)S(1)} %get-tuple-element.58, bf16[4,4,1440,128]{3,2,1,0:T(8,128)(2,1)} %copy-done.2, f32[4,2,1440,128]{3,2,1,0:T(8,128)} %fusion.168, ...), kind=kOutput, calls=%fused_computation.41 | convolution fusion | flops 408453120 | bytes 61972480 | tf_op jit(solution)/shard_map/mrlc,co->mrlo/dot_general | solution.py:45
  68.1 30.4 %collective-permute-start.2 = (bf16[4,1,1440,128]{3,2,1,0:T(8,128)(2,1)S(1)}, bf16[4,1,1440,128]{3,2,1,0:T(8,128)(2,1)S(1)}, u32[]{:S(2)}, u32[]{:S(2)}) collective-permute-start(bf16[4,1,1440,128]{3,2,1,0:T(8,128)(2,1)S(1)} %get-tuple-element.64), channel_id=1, source_target_pairs={{0,1},{1,2},{2,3},{3,4},{4,5},{5,6},{6,7},{8,9},{9,10},{10,11},{11... | collective-permute-start | bytes 4423688 | tf_op jit(solution)/shard_map/ppermute | solution.py:15
  103.7 7.3 %fusion.7 = (bf16[4,4,1441,128]{3,2,1,0:T(8,128)(2,1)S(1)}, bf16[4,4,1441,128]{3,2,1,0:T(8,128)(2,1)S(1)}) fusion(bf16[4,1,1440,128]{3,2,1,0:T(8,128)(2,1)S(1)} %collective-permute-done.3, bf16[4,2,1440,128]{3,2,1,0:T(8,128)(2,1)S(1)} %copy-done.5, bf16[4,1,1440,128]{3,2,1,0:T(8,128)(2,1)S(1)} %collective-permute-done.2), kind=kLoop, calls=%fused_computation.26 | loop fusion | flops 70828032 | bytes 17702912 | tf_op jit(solution)/shard_map/concatenate | solution.py:26
  111.0 4.1 fusion.76
  133.2 8.2 %fusion.71 = bf16[4,69,2,1440]{3,1,2,0:T(8,128)(2,1)} fusion(bf16[4,4,1441,128]{3,2,1,0:T(8,128)(2,1)S(1)} %get-tuple-element.57, f32[4,2,1440,69]{2,3,1,0:T(8,128)S(1)} %fusion.53, f32[4,2,1440,69]{2,3,1,0:T(8,128)} %fusion.76, f32[4,2,1440,69]{2,3,1,0:T(8,128)} %fusion.80, f32[4,2,1440,69]{2,3,1,0:T(8,128)S(1)} %fusion.218, ...), kind=kOutput, calls=%fused_computation.109 | convolution fusion | flops 210643200 | bytes 32868864 | tf_op jit(solution)/shard_map/mrlc,cv->mvrl/dot_general | solution.py:59
  141.4 8.4 %copy.54 = bf16[4,69,2,1440]{1,2,0,3:T(2,128)(2,1)} copy(bf16[4,69,2,1440]{3,1,2,0:T(8,128)(2,1)} %fusion.71) | data formatting | bytes 3179520 | tf_op jit(solution)/shard_map/convert_element_type | solution.py:145
  149.8 4.9 all-to-all-start
  155.2 46.0 %all-to-all-done = bf16[4,69,2,1440]{1,2,0,3:T(2,128)(2,1)} async-done(((bf16[4,69,2,1440]{1,2,0,3:T(2,128)(2,1)}), bf16[4,69,2,1440]{1,2,0,3:T(2,128)(2,1)}, u32[]{:S(2)}, u32[]{:S(2)}) %all-to-all-start) | async-done | bytes 1589792 | tf_op jit(solution)/shard_map/all_to_all | solution.py:150
  201.1 7.7 %copy.55 = bf16[4,69,2,1440]{3,0,2,1:T(4,128)(2,1)S(1)} copy(bf16[4,69,2,1440]{1,2,0,3:T(2,128)(2,1)} %all-to-all-done) | data formatting | bytes 3179520 | tf_op jit(solution)/shard_map/all_to_all | solution.py:150
  208.9 3.8 reshape.78
  212.7 5.6 copy.57
  222.1 61.3 %while.10 = (s32[]{:T(128)}, f32[23,16,3,2,360]{4,1,3,2,0:T(8,128)}, f32[23,16,3,2,360]{4,3,2,0,1:T(2,128)}, f32[23,3]{1,0:T(8,128)S(1)}, s32[]{:T(128)}) while((s32[]{:T(128)}, f32[23,16,3,2,360]{4,1,3,2,0:T(8,128)}, f32[23,16,3,2,360]{4,3,2,0,1:T(2,128)}, f32[23,3]{1,0:T(8,128)S(1)}, s32[]{:T(128)}) %tuple.48), condition=%wide.region_2.3_spmd, body=%wide.region_0.2_spmd.sunk | while | flops 3283202 | bytes 1253493 | solution.py:159
  291.0 25.7 %all_to_all.27 = bf16[16,69,2,360]{3,2,1,0:T(2,128)(2,1)S(1)} all-to-all(bf16[16,69,2,360]{3,2,1,0:T(2,128)(2,1)S(1)} %copy.62), channel_id=1, replica_groups=mesh['mem'=4,'lat'=8] {'mem'}, dimensions={0} | all-to-all | bytes 3179520 | tf_op jit(solution)/shard_map/all_to_all | solution.py:167
  334.7 22.2 %collective-permute-start.4 = (bf16[4,69,1,1440]{3,0,2,1:T(4,128)(2,1)S(1)}, bf16[4,69,1,1440]{3,0,2,1:T(4,128)(2,1)S(1)}, u32[]{:S(2)}, u32[]{:S(2)}) collective-permute-start(bf16[4,69,1,1440]{3,0,2,1:T(4,128)(2,1)S(1)} %copy.65), channel_id=1, source_target_pairs={{0,1},{1,2},{2,3},{3,4},{4,5},{5,6},{6,7},{8,9},{9,10},{10,11},{11... | collective-permute-start | bytes 2384648 | tf_op jit(solution)/shard_map/ppermute | solution.py:15
  364.4 43.1 %collective-permute-done.5 = bf16[4,69,1,1440]{3,0,2,1:T(4,128)(2,1)S(1)} collective-permute-done((bf16[4,69,1,1440]{3,0,2,1:T(4,128)(2,1)S(1)}, bf16[4,69,1,1440]{3,0,2,1:T(4,128)(2,1)S(1)}, u32[]{:S(2)}, u32[]{:S(2)}) %collective-permute-start.5) | collective-permute-done | bytes 794912 | tf_op jit(solution)/shard_map/ppermute | solution.py:17
  407.8 4.2 fusion.98
  412.0 4.2 fusion.95
  416.3 4.1 fusion.104
  420.4 4.1 fusion.108
  424.5 4.2 fusion.101
  428.6 4.0 fusion.57
  436.2 21.4 %fusion.19 = bf16[4,2,1440,128]{3,2,1,0:T(8,128)(2,1)} fusion(f32[4,2,1440,128]{3,2,1,0:T(8,128)} %get-tuple-element.82, f32[4,2,1440,128]{3,2,1,0:T(8,128)} %fusion.61, f32[4,2,1440,128]{3,2,1,0:T(8,128)} %fusion.108, f32[4,2,1440,128]{3,2,1,0:T(8,128)} %fusion.95, f32[4,2,1440,128]{3,2,1,0:T(8,128)} %fusion.216, f32[4,2,1440,128]{3,2,1,0:T(8,128)} %fusion.101, ...), kind=kOutput, calls=%fused_computation.39 | convolution fusion | flops 245007360 | bytes 59526144 | tf_op jit(solution)/shard_map/mvrl,cv->mrlc/dot_general | solution.py:73
  457.6 3.9 fusion.118
  473.5 17.4 %collective-permute-start.6 = (bf16[4,1,1440,128]{3,2,1,0:T(8,128)(2,1)}, bf16[4,1,1440,128]{3,2,1,0:T(8,128)(2,1)}, u32[]{:S(2)}, u32[]{:S(2)}) collective-permute-start(bf16[4,1,1440,128]{3,2,1,0:T(8,128)(2,1)} %get-tuple-element.63), channel_id=1, source_target_pairs={{0,1},{1,2},{2,3},{3,4},{4,5},{5,6},{6,7},{8,9},{9,10},{10,11},{11... | collective-permute-start | bytes 4423688 | tf_op jit(solution)/shard_map/ppermute | solution.py:15
  493.8 5.2 fusion.175
  499.1 122.8 %all-reduce.3.cloned.1.call-done = (f32[3,3,128,128]{3,2,1,0:T(8,128)}, f32[3,3,128,69]{2,3,1,0:T(8,128)}) async-done(((f32[3,3,128,128]{3,2,1,0:T(8,128)}, f32[3,3,128,69]{2,3,1,0:T(8,128)}), (f32[3,3,128,128]{3,2,1,0:T(8,128)}, f32[3,3,128,69]{2,3,1,0:T(8,128)})) %all-reduce.3.cloned.1.call-update) | async-done | bytes 907792 | tf_op jit(solution)/shard_map/psum | solution.py:178
  625.5 7.7 %fusion.4 = (bf16[4,4,1441,128]{3,2,1,0:T(8,128)(2,1)S(1)}, bf16[4,4,1441,128]{3,2,1,0:T(8,128)(2,1)S(1)}) fusion(bf16[4,1,1440,128]{3,2,1,0:T(8,128)(2,1)S(1)} %collective-permute-done.7, bf16[4,2,1440,128]{3,2,1,0:T(8,128)(2,1)} %fusion.19, bf16[4,1,1440,128]{3,2,1,0:T(8,128)(2,1)} %collective-permute-done.6), kind=kLoop, calls=%fused_computation.17 | loop fusion | flops 70828032 | bytes 17702912 | tf_op jit(solution)/shard_map/concatenate | solution.py:26
  633.2 3.9 fusion.45
  651.5 4.8 fusion.24
  659.8 19.4 %add_convert_fusion = bf16[4,2,1440,128]{3,2,1,0:T(8,128)(2,1)} fusion(f32[4,2,1440,128]{3,2,1,0:T(8,128)} %fusion.24, f32[4,2,1440,128]{3,2,1,0:T(8,128)} %fusion.43, f32[4,2,1440,128]{3,2,1,0:T(8,128)} %fusion.45, f32[4,2,1440,128]{3,2,1,0:T(8,128)} %fusion.175, f32[4,2,1440,128]{3,2,1,0:T(8,128)} %fusion.47, f32[4,2,1440,128]{3,2,1,0:T(8,128)} %fusion.49, ...), kind=kOutput, calls=%fused_computation.40 | convolution fusion | flops 390758400 | bytes 53116928 | tf_op jit(solution)/shard_map/mrlo,co->mrlc/dot_general | solution.py:92
  (269 shorter events, 193.1 us)
Async XLA Ops:
  7.2 147.7 %copy-start = (f32[69,2,1440]{2,1,0:T(2,128)S(1)}, f32[69,2,1440]{2,1,0:T(2,128)}, u32[]{:S(2)}) copy-start(f32[69,2,1440]{2,1,0:T(2,128)} %param.11) | copy-start | bytes 2384644
  7.2 6.0 copy-start.9
  7.2 6.0 copy-start.21
  9.4 7.3 %collective-permute-start = (bf16[4,1,1440,128]{3,2,1,0:T(8,128)(2,1)S(1)}, bf16[4,1,1440,128]{3,2,1,0:T(8,128)(2,1)S(1)}, u32[]{:S(2)}, u32[]{:S(2)}) collective-permute-start(bf16[4,1,1440,128]{3,2,1,0:T(8,128)(2,1)S(1)} %get-tuple-element.69), channel_id=1, source_target_pairs={{0,1},{1,2},{2,3},{3,4},{4,5},{5,6},{6,7},{8,9},{9,10},{10,11},{11... | collective-permute-start | bytes 4423688 | tf_op jit(solution)/shard_map/ppermute | solution.py:15
  11.9 7.2 %collective-permute-start.1 = (bf16[4,1,1440,128]{3,2,1,0:T(8,128)(2,1)S(1)}, bf16[4,1,1440,128]{3,2,1,0:T(8,128)(2,1)S(1)}, u32[]{:S(2)}, u32[]{:S(2)}) collective-permute-start(bf16[4,1,1440,128]{3,2,1,0:T(8,128)(2,1)S(1)} %get-tuple-element.70), channel_id=1, source_target_pairs={{1,0},{2,1},{3,2},{4,3},{5,4},{6,5},{7,6},{9,8},{10,9},{11,10},{12... | collective-permute-start | bytes 4423688 | tf_op jit(solution)/shard_map/ppermute | solution.py:17
  19.0 22.4 %copy-start.15 = (bf16[4,3,1440,128]{3,2,1,0:T(8,128)(2,1)}, bf16[4,3,1440,128]{3,2,1,0:T(8,128)(2,1)S(1)}, u32[]{:S(2)}) copy-start(bf16[4,3,1440,128]{3,2,1,0:T(8,128)(2,1)S(1)} %get-tuple-element.66) | copy-start | bytes 13271044
  19.6 14.9 %copy-start.2 = (bf16[4,4,1440,128]{3,2,1,0:T(8,128)(2,1)}, bf16[4,4,1440,128]{3,2,1,0:T(8,128)(2,1)S(1)}, u32[]{:S(2)}) copy-start(bf16[4,4,1440,128]{3,2,1,0:T(8,128)(2,1)S(1)} %get-tuple-element.75) | copy-start | bytes 17694724
  19.6 18.3 %copy-start.13 = (bf16[4,3,1440,128]{3,2,1,0:T(8,128)(2,1)}, bf16[4,3,1440,128]{3,2,1,0:T(8,128)(2,1)S(1)}, u32[]{:S(2)}) copy-start(bf16[4,3,1440,128]{3,2,1,0:T(8,128)(2,1)S(1)} %get-tuple-element.76) | copy-start | bytes 13271044
  66.0 34.1 %copy-start.5 = (bf16[4,2,1440,128]{3,2,1,0:T(8,128)(2,1)S(1)}, bf16[4,2,1440,128]{3,2,1,0:T(8,128)(2,1)}, u32[]{:S(2)}) copy-start(bf16[4,2,1440,128]{3,2,1,0:T(8,128)(2,1)} %get-tuple-element.81) | copy-start | bytes 8847364
  66.0 34.1 %copy-start.22 = (bf16[3,3,128,69]{2,3,1,0:T(8,128)(2,1)S(1)}, bf16[3,3,128,69]{2,3,1,0:T(8,128)(2,1)}, u32[]{:S(2)}) copy-start(bf16[3,3,128,69]{2,3,1,0:T(8,128)(2,1)} %param.10) | copy-start | bytes 476932
  68.1 33.7 %collective-permute-start.2 = (bf16[4,1,1440,128]{3,2,1,0:T(8,128)(2,1)S(1)}, bf16[4,1,1440,128]{3,2,1,0:T(8,128)(2,1)S(1)}, u32[]{:S(2)}, u32[]{:S(2)}) collective-permute-start(bf16[4,1,1440,128]{3,2,1,0:T(8,128)(2,1)S(1)} %get-tuple-element.64), channel_id=1, source_target_pairs={{0,1},{1,2},{2,3},{3,4},{4,5},{5,6},{6,7},{8,9},{9,10},{10,11},{11... | collective-permute-start | bytes 4423688 | tf_op jit(solution)/shard_map/ppermute | solution.py:15
  98.5 5.2 collective-permute-start.3
  101.9 29.5 %copy-start.19 = (bf16[4,1,1440,128]{3,2,1,0:T(8,128)(2,1)}, bf16[4,1,1440,128]{3,2,1,0:T(8,128)(2,1)S(1)}, u32[]{:S(2)}) copy-start(bf16[4,1,1440,128]{3,2,1,0:T(8,128)(2,1)S(1)} %collective-permute-done.2) | copy-start | bytes 4423684
  103.7 25.8 %copy-start.17 = (bf16[4,1,1440,128]{3,2,1,0:T(8,128)(2,1)}, bf16[4,1,1440,128]{3,2,1,0:T(8,128)(2,1)S(1)}, u32[]{:S(2)}) copy-start(bf16[4,1,1440,128]{3,2,1,0:T(8,128)(2,1)S(1)} %collective-permute-done.3) | copy-start | bytes 4423684
  111.0 7.7 %copy-start.12 = (bf16[4,4,1441,128]{3,2,1,0:T(8,128)(2,1)}, bf16[4,4,1441,128]{3,2,1,0:T(8,128)(2,1)S(1)}, u32[]{:S(2)}) copy-start(bf16[4,4,1441,128]{3,2,1,0:T(8,128)(2,1)S(1)} %get-tuple-element.56) | copy-start | bytes 17707012
  111.0 22.2 %copy-start.11 = (bf16[4,4,1441,128]{3,2,1,0:T(8,128)(2,1)}, bf16[4,4,1441,128]{3,2,1,0:T(8,128)(2,1)S(1)}, u32[]{:S(2)}) copy-start(bf16[4,4,1441,128]{3,2,1,0:T(8,128)(2,1)S(1)} %get-tuple-element.57) | copy-start | bytes 17707012
  141.4 13.4 %copy-start.26 = (f32[69]{0:T(128)S(1)}, f32[69]{0:T(128)}, u32[]{:S(2)}) copy-start(f32[69]{0:T(128)} %param.13) | copy-start | bytes 832
  141.4 13.4 %copy-start.27 = (f32[69]{0:T(128)S(1)}, f32[69]{0:T(128)}, u32[]{:S(2)}) copy-start(f32[69]{0:T(128)} %param.12) | copy-start | bytes 832
  149.8 51.3 %all-to-all-start = ((bf16[4,69,2,1440]{1,2,0,3:T(2,128)(2,1)}), bf16[4,69,2,1440]{1,2,0,3:T(2,128)(2,1)}, u32[]{:S(2)}, u32[]{:S(2)}) async-start(bf16[4,69,2,1440]{1,2,0,3:T(2,128)(2,1)} %copy.54), calls=%async_computation | async-start | bytes 5898240 | tf_op jit(solution)/shard_map/all_to_all | solution.py:150
  154.7 467.1 %all-reduce.3.cloned.1.call-start = ((), (), s32[]{:S(2)}) async-start(), calls=%async_computation.2 | async-start | bytes 1843200 | tf_op jit(solution)/shard_map/psum | solution.py:178
  212.7 5.6 copy-start.14
  333.1 25.3 %copy-start.18 = (bf16[4,1,1440,128]{3,2,1,0:T(8,128)(2,1)S(1)}, bf16[4,1,1440,128]{3,2,1,0:T(8,128)(2,1)}, u32[]{:S(2)}) copy-start(bf16[4,1,1440,128]{3,2,1,0:T(8,128)(2,1)} %copy-done.17) | copy-start | bytes 4423684
  334.7 29.3 %collective-permute-start.4 = (bf16[4,69,1,1440]{3,0,2,1:T(4,128)(2,1)S(1)}, bf16[4,69,1,1440]{3,0,2,1:T(4,128)(2,1)S(1)}, u32[]{:S(2)}, u32[]{:S(2)}) collective-permute-start(bf16[4,69,1,1440]{3,0,2,1:T(4,128)(2,1)S(1)} %copy.65), channel_id=1, source_target_pairs={{0,1},{1,2},{2,3},{3,4},{4,5},{5,6},{6,7},{8,9},{9,10},{10,11},{11... | collective-permute-start | bytes 2384648 | tf_op jit(solution)/shard_map/ppermute | solution.py:15
  356.9 50.5 %collective-permute-start.5 = (bf16[4,69,1,1440]{3,0,2,1:T(4,128)(2,1)S(1)}, bf16[4,69,1,1440]{3,0,2,1:T(4,128)(2,1)S(1)}, u32[]{:S(2)}, u32[]{:S(2)}) collective-permute-start(bf16[4,69,1,1440]{3,0,2,1:T(4,128)(2,1)S(1)} %copy.66), channel_id=1, source_target_pairs={{1,0},{2,1},{3,2},{4,3},{5,4},{6,5},{7,6},{9,8},{10,9},{11,10},{12... | collective-permute-start | bytes 2384648 | tf_op jit(solution)/shard_map/ppermute | solution.py:17
  407.6 16.8 %copy-start.7 = (bf16[4,69,4,1440]{3,1,2,0:T(8,128)(2,1)}, bf16[4,69,4,1440]{3,1,2,0:T(8,128)(2,1)S(1)}, u32[]{:S(2)}) copy-start(bf16[4,69,4,1440]{3,1,2,0:T(8,128)(2,1)S(1)} %get-tuple-element.78) | copy-start | bytes 9538564
  457.6 8.6 %slice-start = ((s8[5898240]{0:T(1024)(128)(4,1)}), s8[4194304]{0:T(1024)(128)(4,1)S(1)}, s32[]{:S(2)}) async-start(s8[5898240]{0:T(1024)(128)(4,1)} %bitcast.371), calls=%async_computation.3 | async-start | bytes 8388608
  461.6 4.6 slice-start.1
  469.1 21.9 %slice-start.6 = ((s8[4423680]{0:T(1024)(128)(4,1)}), s8[4194304]{0:T(1024)(128)(4,1)S(1)}, s32[]{:S(2)}) async-start(s8[4423680]{0:T(1024)(128)(4,1)} %bitcast.377), calls=%async_computation.9 | async-start | bytes 8388608
  470.1 20.8 %slice-start.7 = ((s8[4423680]{0:T(1024)(128)(4,1)}), s8[229376]{0:T(1024)(128)(4,1)S(1)}, s32[]{:S(2)}) async-start(s8[4423680]{0:T(1024)(128)(4,1)} %bitcast.377), calls=%async_computation.10 | async-start | bytes 458752
  472.2 153.3 %collective-permute-start.7 = (bf16[4,1,1440,128]{3,2,1,0:T(8,128)(2,1)}, bf16[4,1,1440,128]{3,2,1,0:T(8,128)(2,1)S(1)}, u32[]{:S(2)}, u32[]{:S(2)}) collective-permute-start(bf16[4,1,1440,128]{3,2,1,0:T(8,128)(2,1)} %get-tuple-element.62), channel_id=1, source_target_pairs={{1,0},{2,1},{3,2},{4,3},{5,4},{6,5},{7,6},{9,8},{10,9},{11,10},{12... | collective-permute-start | bytes 4423688 | tf_op jit(solution)/shard_map/ppermute | solution.py:17
  473.5 152.0 %collective-permute-start.6 = (bf16[4,1,1440,128]{3,2,1,0:T(8,128)(2,1)}, bf16[4,1,1440,128]{3,2,1,0:T(8,128)(2,1)}, u32[]{:S(2)}, u32[]{:S(2)}) collective-permute-start(bf16[4,1,1440,128]{3,2,1,0:T(8,128)(2,1)} %get-tuple-element.63), channel_id=1, source_target_pairs={{0,1},{1,2},{2,3},{3,4},{4,5},{5,6},{6,7},{8,9},{9,10},{10,11},{11... | collective-permute-start | bytes 4423688 | tf_op jit(solution)/shard_map/ppermute | solution.py:15
  659.8 19.4 %copy-start.1 = (f32[69,2,1440]{2,1,0:T(2,128)S(1)}, f32[69,2,1440]{2,1,0:T(2,128)}, u32[]{:S(2)}) copy-start(f32[69,2,1440]{2,1,0:T(2,128)} %param.11) | copy-start | bytes 2384644
  (14 other events, 38.6 us)
Sparse Core Ops, SparseCore 0:
  494.0 127.8 all-reduce.2
where the time goes:
time: 697 us; the launch traced here: 686 us
  waiting for transfers between devices  214 us (31%)
  matrix products  210 us (30%)
  local copies, waits for them, and re-layouts  90.5 us (13%)
  starting transfers between devices  82.9 us (12%)
  other arithmetic  47.9 us (7%)
  blocking collectives  25.7 us (4%)
  between operations  14.9 us (2%)
    psum x1, waiting for transfers between devices, shards(): inner_sum, head_sum = lax.psum((inner_grad, head_grad), ('mem', 'lat'))  123 us
    ppermute x4, starting transfers between devices, padded_2(): lax.ppermute(tail, axis, [(i, (i + 1) % count) for i in range(ends)])  72.5 us
    dot_general x9, matrix products, field_back(): jnp.einsum('mvrl,cv->mrlc', padded_grad[:, :, 2 - row_off:2 - row_off + b...  53.3 us
    dot_general x9, matrix products, hidden_back(): jnp.einsum('mrlo,co->mrlc', padded_grad[:, 2 - row_off:2 - row_off + band...  50.8 us
    dot_general x9, matrix products, hidden_conv(): jnp.einsum('mrlc,co->mrlo', padded[:, row_off:row_off + band_rows, col_of...  49.8 us
    all_to_all x1, waiting for transfers between devices, shards(): lax.all_to_all(field, 'mem', split_axis=3, concat_axis=0, tiled=True)  46 us
    ppermute x4, waiting for transfers between devices, padded_2(): lax.ppermute(head, axis, [((i + 1) % count, i) for i in range(ends)])  44.9 us
    dot_general x9, matrix products, field_conv(): jnp.einsum('mrlc,cv->mvrl', padded[:, row_off:row_off + band_rows, col_of...  32.1 us
  transfers between devices with their start and end apart: 10, of which 4 were waited for; matrix products, arithmetic and copies ran while one was open for 4% of the time, Pallas kernels for 0%

commit v1 on v0

v1 whole, which is shorter than its diff:
```python
import functools
import math

import jax
import jax.numpy as jnp
from jax import lax
from jax.experimental import pallas as pl
from jax.experimental.pallas import tpu as pltpu
from jax.sharding import PartitionSpec as P

BF16 = jnp.bfloat16
F32 = jnp.float32
LANES = 128
EDGE = 8
VMEM_LIMIT = 60 * 1024 * 1024


def tile_of(count, step, most):
    return max(t for t in range(step, most + 1, step) if count % t == 0)


def shifted(ref, start, tile, first, count, offsets=(-1, 0, 1)):
    window = ref[pl.ds(start, tile + 2 * EDGE), first : first + count]
    return jnp.concatenate(
        [window[EDGE + off : EDGE + off + tile].astype(BF16) for off in offsets], axis=1
    )


def wrap_edges(ref, lon):
    ref[0:EDGE] = ref[lon : lon + EDGE]
    ref[lon + EDGE : lon + 2 * EDGE] = ref[EDGE : 2 * EDGE]


def forward_kernel(dims, flags, own, top, bot, w_inner, w_head, hidden_out, slope_out, field_out, xs, hs, fs):
    rows, lon, lon_pad, ch, qp, pieces, piece = dims
    tile = tile_of(lon, 16, 480)
    half = math.sqrt(2.0 / math.pi)
    for j in range(rows + 4):
        if j < 2:
            row = top[0, j]
        elif j < rows + 2:
            row = own[0, j - 2]
        else:
            row = bot[0, j - rows - 2]
        xs[EDGE : EDGE + lon, j * ch : (j + 1) * ch] = row.astype(F32)
    wrap_edges(xs, lon)
    top_ok = flags[0].astype(F32)
    bot_ok = flags[1].astype(F32)

    def inner_step(t, carry):
        start = pl.multiple_of(t * tile, tile)
        for p in range((rows + 2) // 2):
            patch = shifted(xs, start, tile, 2 * p * ch, 4 * ch)
            pre = jnp.dot(patch, w_inner[...], preferred_element_type=F32)
            square = pre * pre
            tanh = jnp.tanh(half * (pre * (1.0 + 0.044715 * square)))
            upper = 0.5 + 0.5 * tanh
            hidden = pre * upper
            slope = upper + (0.5 * half) * pre * (1.0 - tanh * tanh) * (1.0 + (3 * 0.044715) * square)
            for k in range(2):
                i = 2 * p + k
                h = hidden[:, k * ch : (k + 1) * ch]
                s = slope[:, k * ch : (k + 1) * ch]
                if i == 0:
                    h, s = h * top_ok, s * top_ok
                if i == rows + 1:
                    h, s = h * bot_ok, s * bot_ok
                hs[pl.ds(start + EDGE, tile), i * ch : (i + 1) * ch] = h
                slope_out[0, i, pl.ds(start, tile), :] = s.astype(BF16)
                if 1 <= i <= rows:
                    hidden_out[0, i - 1, pl.ds(start, tile), :] = h.astype(BF16)
        return carry

    lax.fori_loop(0, lon // tile, inner_step, 0)
    wrap_edges(hs, lon)
    zero = jnp.zeros((lon_pad - lon, ch), BF16)
    for i in range(rows + 2):
        slope_out[0, i, lon:lon_pad, :] = zero
    for i in range(rows):
        hidden_out[0, i, lon:lon_pad, :] = zero

    def head_step(t, carry):
        start = pl.multiple_of(t * tile, tile)
        for g in range(rows // 2):
            patch = shifted(hs, start, tile, 2 * g * ch, 4 * ch)
            fs[g, pl.ds(start, tile), :] = jnp.dot(patch, w_head[...], preferred_element_type=F32)
        return carry

    lax.fori_loop(0, lon // tile, head_step, 0)
    pair = qp // (rows // 2)
    for g in range(rows // 2):
        fs[g, lon:lon_pad, :] = jnp.zeros((lon_pad - lon, fs.shape[2]), F32)
        fs[g, lon : lon + EDGE, :] = fs[g, 0:EDGE, :]
        fs[g, lon_pad - EDGE : lon_pad, :] = fs[g, lon - EDGE : lon, :]
        for j in range(pieces):
            turned = fs[g, j * piece : (j + 1) * piece, :].T
            field_out[j, 0, g * pair : (g + 1) * pair, :] = turned[:pair].astype(BF16)


def pair_kernel(dims, fields, truth, rate, scale, out, vals, accs):
    members, per, sub, piece = dims
    norm = 2.0 / (members - 1)

    for m in range(members):
        vals[m] = fields[m // per, m % per].astype(F32)
    blocks = piece // LANES

    def step(t, carry):
        r = pl.ds(pl.multiple_of((t // blocks) * 8, 8), 8)
        c = pl.ds(pl.multiple_of((t % blocks) * LANES, LANES), LANES)
        neg = rate[r, :]
        x = [vals[m, r, c] for m in range(members)]
        sums = [None] * members
        for i in range(members):
            for j in range(i + 1, members):
                d = x[j] - x[i]
                w = jnp.exp2(d * d * neg) * d
                sums[i] = w if sums[i] is None else sums[i] + w
                sums[j] = -w if sums[j] is None else sums[j] - w
        y = truth[r, c]
        sc = scale[r, :]
        for i in range(members):
            off = x[i] - y
            near = jnp.exp2(off * off * neg) * off
            accs[i, r, c] = sc * (norm * sums[i] + 2.0 * near)
        return carry

    lax.fori_loop(0, (sub // 8) * blocks, step, 0)
    for m in range(members):
        out[m // per, m % per] = accs[m].astype(BF16)


def backward_kernel(dims, own, top, bot, hidden, slope, feats, w_back, w_grad, grad_out, sums_out, gs, ss, acc_in, acc_hd):
    rows, lon, lon_pad, ch, vp, pieces, piece, low, span = dims
    ext = (rows + 4) * vp
    step_m = pl.program_id(0)

    @pl.when(step_m == 0)
    def _():
        acc_in[...] = jnp.zeros_like(acc_in)
        acc_hd[...] = jnp.zeros_like(acc_hd)

    for j in range(pieces):
        cols = slice(j * piece, (j + 1) * piece)
        gs[1, 0 : 2 * vp, cols] = top[j, 0]
        gs[1, 2 * vp : ext - 2 * vp, cols] = own[j, 0]
        gs[1, ext - 2 * vp : ext, cols] = bot[j, 0]

    def roll_step(t, carry):
        r = pl.ds(pl.multiple_of(t * 16, 16), 16)
        block = gs[1, r, :].astype(F32)
        gs[0, r, :] = pltpu.roll(block, lon_pad - 1, 1).astype(BF16)
        gs[2, r, :] = pltpu.roll(block, 1, 1).astype(BF16)
        return carry

    lax.fori_loop(0, ext // 16, roll_step, 0)
    tile = tile_of(lon_pad, LANES, 512)

    def hidden_step(t, carry):
        start = pl.multiple_of(t * tile, tile)
        for p in range((rows + 2) // 2):
            patch = jnp.concatenate(
                [gs[b, 2 * p * vp : (2 * p + 4) * vp, pl.ds(start, tile)] for b in range(3)], axis=0
            )
            back = lax.dot_general(
                patch, w_back[...], (((0,), (0,)), ((), ())), preferred_element_type=F32
            )
            for k in range(2):
                i = 2 * p + k
                ss[pl.ds(start + EDGE, tile), i * ch : (i + 1) * ch] = back[
                    :, k * ch : (k + 1) * ch
                ] * slope[0, i, pl.ds(start, tile), :].astype(F32)
        for g in range(rows // 2):
            base = 2 * g * vp + low
            patch = jnp.concatenate(
                [gs[b, base : base + span, pl.ds(start, tile)] for b in range(3)], axis=0
            )
            act = jnp.concatenate(
                [hidden[0, 2 * g + k, pl.ds(start, tile), :] for k in range(2)], axis=1
            )
            acc_hd[...] += jnp.dot(patch, act, preferred_element_type=F32)
        return carry

    lax.fori_loop(0, lon_pad // tile, hidden_step, 0)
    wrap_edges(ss, lon)
    tile2 = tile_of(lon, 16, 480)

    def feature_step(t, carry):
        start = pl.multiple_of(t * tile2, tile2)
        for g in range(rows // 2):
            patch = shifted(ss, start, tile2, 2 * g * ch, 4 * ch, (1, 0, -1))
            grad = jnp.dot(patch, w_grad[...], preferred_element_type=F32)
            for k in range(2):
                grad_out[0, 2 * g + k, pl.ds(start, tile2), :] = grad[
                    :, k * ch : (k + 1) * ch
                ].astype(BF16)
            act = jnp.concatenate(
                [feats[0, 2 * g + k, pl.ds(start, tile2), :] for k in range(2)], axis=1
            )
            acc_in[...] += lax.dot_general(
                act, patch, (((0,), (0,)), ((), ())), preferred_element_type=F32
            )
        return carry

    lax.fori_loop(0, lon // tile2, feature_step, 0)

    @pl.when(step_m == pl.num_programs(0) - 1)
    def _():
        for a in range(3):
            for b in range(3):
                inner = None
                head = None
                for k in range(2):
                    n = k + 2 - a
                    part = acc_in[k * ch : (k + 1) * ch, (b * 4 + n) * ch : (b * 4 + n + 1) * ch]
                    inner = part if inner is None else inner + part
                    n = k + 3 - a
                    at = b * span + n * vp - low
                    part = acc_hd[at : at + vp, k * ch : (k + 1) * ch]
                    head = part if head is None else head + part
                q = 3 * a + b
                sums_out[q * ch : (q + 1) * ch, :] = inner
                at = 9 * ch + q * vp
                sums_out[at : at + vp, :] = head


def forward_weights(kernel, width):
    ch, outs = kernel.shape[2], kernel.shape[3]
    kernel = jnp.pad(kernel, ((0, 0), (0, 0), (0, 0), (0, width - outs)))
    cols = []
    for out_row in range(2):
        taps = jnp.pad(kernel, ((out_row, 1 - out_row), (0, 0), (0, 0), (0, 0)))
        cols.append(jnp.moveaxis(taps, 0, 1))
    return jnp.stack(cols, axis=3).reshape(3 * 4 * ch, 2 * width)


def backward_weights(kernel, width):
    ch, outs = kernel.shape[2], kernel.shape[3]
    kernel = jnp.pad(kernel, ((0, 0), (0, 0), (0, 0), (0, width - outs)))[::-1]
    cols = []
    for out_row in range(2):
        taps = jnp.pad(kernel, ((out_row, 1 - out_row), (0, 0), (0, 0), (0, 0)))
        cols.append(jnp.transpose(taps, (1, 0, 3, 2)))
    return jnp.stack(cols, axis=3).reshape(3 * 4 * width, 2 * ch)


def neighbours(tail, head, axis):
    count = lax.axis_size(axis)
    before = lax.ppermute(tail, axis, [(i, i + 1) for i in range(count - 1)])
    after = lax.ppermute(head, axis, [(i + 1, i) for i in range(count - 1)])
    return before, after


def reduce_all(values, axes):
    count = math.prod(lax.axis_size(a) for a in axes)
    rows, width = values.shape
    part = -(-rows // (16 * count)) * 16
    padded = jnp.pad(values, ((0, part * count - rows), (0, 0))).astype(BF16)
    got = lax.all_to_all(padded, axes, 0, 0, tiled=True)
    summed = jnp.sum(got.reshape(count, part, width).astype(F32), axis=0).astype(BF16)
    spread = jnp.broadcast_to(summed[None], (count, part, width))
    full = lax.all_to_all(spread, axes, 0, 0)
    return full.reshape(count * part, width)[:rows].astype(F32)


def shards(features, conv_inner, conv_head, truth, kernel_width, var_weight):
    per, rows, lon, ch = features.shape
    variables = conv_head.shape[3]
    pieces = lax.axis_size("mem")
    members = per * pieces
    vp = -(-variables // 8) * 8
    qp = rows * vp
    piece = -(-lon // (LANES * pieces)) * LANES
    if lon + 2 * EDGE > piece * pieces:
        piece += LANES
    lon_pad = piece * pieces
    assert rows % 2 == 0 and lon % 16 == 0 and (2 * vp) % 16 == 0 and 2 * vp <= 256
    low = vp // 16 * 16
    span = -(-(5 * vp - low) // 16) * 16

    top, bot = neighbours(features[:, rows - 2 :], features[:, :2], "lat")
    at = lax.axis_index("lat")
    flags = jnp.stack([at > 0, at < lax.axis_size("lat") - 1]).astype(jnp.int32)

    w_inner = forward_weights(conv_inner, ch)
    w_head = jnp.pad(forward_weights(conv_head, vp), ((0, 0), (0, 256 - 2 * vp)))
    w_back = backward_weights(conv_head, vp)
    w_grad = backward_weights(conv_inner, ch)

    params = functools.partial(pltpu.CompilerParams, vmem_limit_bytes=VMEM_LIMIT)
    whole = lambda shape: pl.BlockSpec(shape, lambda m: (0,) * len(shape))
    member = lambda shape: pl.BlockSpec((1,) + shape, lambda m: (m,) + (0,) * len(shape))
    spread = lambda n: pl.BlockSpec((pieces, 1, n, piece), lambda m: (0, m, 0, 0))

    macs = 2 * lon * 12 * ch * 2 * ch * per
    hidden, slope, field = pl.pallas_call(
        functools.partial(forward_kernel, (rows, lon, lon_pad, ch, qp, pieces, piece)),
        grid=(per,),
        in_specs=[
            pl.BlockSpec(memory_space=pltpu.SMEM),
            member((rows, lon, ch)),
            member((2, lon, ch)),
            member((2, lon, ch)),
            whole(w_inner.shape),
            whole(w_head.shape),
        ],
        out_specs=[member((rows, lon_pad, ch)), member((rows + 2, lon_pad, ch)), spread(qp)],
        out_shape=[
            jax.ShapeDtypeStruct((per, rows, lon_pad, ch), BF16),
            jax.ShapeDtypeStruct((per, rows + 2, lon_pad, ch), BF16),
            jax.ShapeDtypeStruct((pieces, per, qp, piece), BF16),
        ],
        scratch_shapes=[
            pltpu.VMEM((lon + 2 * EDGE, (rows + 4) * ch), F32),
            pltpu.VMEM((lon + 2 * EDGE, (rows + 2) * ch), F32),
            pltpu.VMEM((rows // 2, lon_pad, 256), F32),
        ],
        compiler_params=params(),
        cost_estimate=pl.CostEstimate(flops=3 * macs, bytes_accessed=24 << 20, transcendentals=0),
        name="forward",
    )(flags, features, top, bot, w_inner, w_head)

    traded = lax.all_to_all(field, "mem", 0, 0, tiled=True)

    truth_rows = jnp.moveaxis(truth, 1, 0)
    truth_rows = jnp.pad(truth_rows, ((0, 0), (0, vp - variables), (0, 0))).reshape(qp, lon)
    middle = jnp.zeros((qp, lon_pad - lon - 2 * EDGE), F32)
    truth_rows = jnp.concatenate(
        [truth_rows, truth_rows[:, :EDGE], middle, truth_rows[:, lon - EDGE :]], axis=1
    )
    truth_piece = lax.dynamic_slice_in_dim(truth_rows, lax.axis_index("mem") * piece, piece, 1)
    inverse = 1.0 / (kernel_width * kernel_width)
    spread_param = lambda v: jnp.broadcast_to(
        jnp.tile(jnp.pad(v, (0, vp - variables)), rows)[:, None], (qp, LANES)
    )
    rate = spread_param((-0.5 * math.log2(math.e)) * inverse)
    scale = spread_param(var_weight * inverse)
    sub = 16
    row_block = lambda width: pl.BlockSpec((sub, width), lambda i: (i, 0))
    field_block = pl.BlockSpec((pieces, per, sub, piece), lambda i: (0, 0, i, 0))
    gradient = pl.pallas_call(
        functools.partial(pair_kernel, (members, per, sub, piece)),
        grid=(qp // sub,),
        in_specs=[field_block, row_block(piece), row_block(LANES), row_block(LANES)],
        out_specs=field_block,
        out_shape=jax.ShapeDtypeStruct(traded.shape, BF16),
        scratch_shapes=[pltpu.VMEM((members, sub, piece), F32)] * 2,
        compiler_params=params(),
        cost_estimate=pl.CostEstimate(
            flops=4 * members * members * qp * piece,
            bytes_accessed=4 * members * qp * piece,
            transcendentals=members * members // 2 * qp * piece,
        ),
        name="pairs",
    )(traded, truth_piece, rate, scale)

    own = lax.all_to_all(gradient, "mem", 0, 0, tiled=True)
    g_top, g_bot = neighbours(own[:, :, qp - 2 * vp :], own[:, :, : 2 * vp], "lat")
    sums_rows = 9 * (ch + vp)
    grad_features, sums = pl.pallas_call(
        functools.partial(backward_kernel, (rows, lon, lon_pad, ch, vp, pieces, piece, low, span)),
        grid=(per,),
        in_specs=[
            spread(qp),
            spread(2 * vp),
            spread(2 * vp),
            member((rows, lon_pad, ch)),
            member((rows + 2, lon_pad, ch)),
            member((rows, lon, ch)),
            whole(w_back.shape),
            whole(w_grad.shape),
        ],
        out_specs=[member((rows, lon, ch)), whole((sums_rows, ch))],
        out_shape=[
            jax.ShapeDtypeStruct(features.shape, BF16),
            jax.ShapeDtypeStruct((sums_rows, ch), F32),
        ],
        scratch_shapes=[
            pltpu.VMEM((3, (rows + 4) * vp, lon_pad), BF16),
            pltpu.VMEM((lon_pad + 2 * EDGE, (rows + 2) * ch), F32),
            pltpu.VMEM((2 * ch, 12 * ch), F32),
            pltpu.VMEM((3 * span, 2 * ch), F32),
        ],
        compiler_params=params(),
        cost_estimate=pl.CostEstimate(flops=5 * macs, bytes_accessed=24 << 20, transcendentals=0),
        name="backward",
    )(own, g_top, g_bot, hidden, slope, features, w_back, w_grad)

    total = reduce_all(sums, ("mem", "lat"))
    points = rows * lax.axis_size("lat") * lon
    inner_sum = total[: 9 * ch].reshape(3, 3, ch, ch)
    head_sum = total[9 * ch :].reshape(3, 3, vp, ch)[:, :, :variables]
    return (grad_features, inner_sum / points, jnp.swapaxes(head_sum, 2, 3) / points)


def solution(mesh):
    in_specs = (P("mem", "lat", None, None), P(), P(), P(None, "lat", None), P(), P())
    out_specs = (P("mem", "lat", None, None), P(), P())
    return jax.shard_map(shards, mesh=mesh, in_specs=in_specs, out_specs=out_specs, check_vma=False)
```

time: 697 us -> 327 us (0.47); the launches traced: 686 us -> 327 us
  matrix products: 210 us -> 0 us
  waiting for transfers between devices: 214 us -> 58.6 us
  Pallas kernels: 0 us -> 82.6 us
  local copies, waits for them, and re-layouts: 90.5 us -> 13 us
  blocking collectives: 25.7 us -> 102 us
  other arithmetic: 47.9 us -> 3.84 us
  starting transfers between devices: 82.9 us -> 66.1 us
  between operations: 14.9 us -> 0.91 us
    dot_general x54 -> x0, matrix products: 210 us -> none  [the longest x9 53.3 us: field_back(): jnp.einsum('mvrl,cv->mrlc', padded_grad[:, :, 2 - row_off:2 - row_off + b...]
    psum x1 -> x0, waiting for transfers between devices: 123 us -> none  [shards(): inner_sum, head_sum = lax.psum((inner_grad, head_grad), ('mem', 'lat'))]
    pallas_call x0 -> x3, Pallas kernels: none -> 82.6 us  [the longest x1 39.3 us: shards(): pl.pallas_call(functools.partial(backward_kernel, (rows, lon, lon_pad, ch...]
    all_to_all x1 -> x3, blocking collectives: 25.7 us -> 102 us  [the longest x1 50 us: reduce_all(): got = lax.all_to_all(padded, axes, 0, 0, tiled=True)]
    all_to_all x1, waiting for transfers between devices: 46 us -> 20.4 us  [shards(): traded = lax.all_to_all(field, 'mem', 0, 0, tiled=True)]
    reduce_sum x23 -> x1, other arithmetic: 23.5 us -> 0.09 us  [reduce_all(): jnp.sum(got.reshape(count, part, width).astype(F32), axis=0).astype(BF16)]
    sub x46 -> x0, local copies, waits for them, and re-layouts: 22 us -> none  [pair_sums(): spread = others[None] - own[:, None]]
    ppermute x8 -> x4, starting transfers between devices: 78 us -> 60.8 us  [the longest x2 58.3 us: neighbours(): before = lax.ppermute(tail, axis, [(i, i + 1) for i in range(count - 1)])]
  transfers between devices with their start and end apart: 10 -> 5, of which waited for: 4 -> 3; matrix products, arithmetic and copies ran while one was open for 4% -> 4% of each run, Pallas kernels for 0% -> 0%
where the time goes in v1:
time: 327 us
  blocking collectives  102 us (31%)
  Pallas kernels  82.6 us (25%)
  starting transfers between devices  66.1 us (20%)
  waiting for transfers between devices  58.6 us (18%)
  local copies, waits for them, and re-layouts  13 us (4%)
  other arithmetic  3.84 us (1%)
    ppermute x2, starting transfers between devices, neighbours(): before = lax.ppermute(tail, axis, [(i, i + 1) for i in range(count - 1)])  58.3 us
    all_to_all x1, blocking collectives, reduce_all(): got = lax.all_to_all(padded, axes, 0, 0, tiled=True)  50 us
    pallas_call x1, Pallas kernels, shards(): pl.pallas_call(functools.partial(backward_kernel, (rows, lon, lon_pad, ch...  39.3 us
    ppermute x2, waiting for transfers between devices, neighbours(): after = lax.ppermute(head, axis, [(i + 1, i) for i in range(count - 1)])  38.3 us
    all_to_all x1, blocking collectives, shards(): own = lax.all_to_all(gradient, 'mem', 0, 0, tiled=True)  33.1 us
    pallas_call x1, Pallas kernels, shards(): pl.pallas_call(functools.partial(forward_kernel, (rows, lon, lon_pad, ch,...  32.6 us
    all_to_all x1, waiting for transfers between devices, shards(): traded = lax.all_to_all(field, 'mem', 0, 0, tiled=True)  20.4 us
    all_to_all x1, blocking collectives, reduce_all(): full = lax.all_to_all(spread, axes, 0, 0)  18.4 us
  transfers between devices with their start and end apart: 5, of which 3 were waited for; matrix products, arithmetic and copies ran while one was open for 4% of the time, Pallas kernels for 0%

profile of v1, /device:TPU:0, one launch (start us, length us, event | category | flops | bytes accessed | tf_op | source)
XLA Modules:
  0.0 326.6 jit_solution(105810491845044087)
XLA Ops:
  0.6 4.0 %collective-permute-start = (bf16[4,2,1440,128]{3,2,1,0:T(8,128)(2,1)}, bf16[4,2,1440,128]{3,2,1,0:T(8,128)(2,1)}, u32[]{:S(2)}, u32[]{:S(2)}) collective-permute-start(bf16[4,2,1440,128]{3,2,1,0:T(8,128)(2,1)} %feats.1), channel_id=1, source_target_pairs={{0,1},{1,2},{2,3},{3,4},{4,5},{5,6},{6,7},{8,9},{9,10},{10,11},{11... | collective-permute-start | bytes 8847368 | tf_op jit(solution)/shard_map/ppermute | solution.py:249
  4.6 1.3 collective-permute-start.1
  5.9 0.9 pad.55
  7.0 0.6 copy.20
  7.6 0.5 reshape.46
  8.0 1.0 pad.58.w_head
  9.3 0.8 copy.14
  10.1 1.0 copy.30
  11.1 0.6 add_convert_fusion.flags
  11.7 1.0 collective-permute-done.1.bot
  12.8 32.6 %forward.1 = (bf16[4,2,1536,128]{3,2,1,0:T(8,128)(2,1)}, bf16[4,4,1536,128]{3,2,1,0:T(8,128)(2,1)}, bf16[4,4,144,384]{3,2,1,0:T(8,128)(2,1)}) custom-call(s32[2]{0:T(128)} %add_convert_fusion.flags, bf16[4,2,1440,128]{3,2,1,0:T(8,128)(2,1)} %feats.1, bf16[4,2,1440,128]{3,2,1,0:T(8,128)(2,1)} %collective-permute-done.top, ...), custom_call_target="tpu_custom_call" | custom-call | flops 13589544960 | bytes 25165824 | tf_op jit(solution)/shard_map/forward/pallas_call | solution.py:296
  45.4 5.3 %all-to-all-start = ((bf16[4,4,144,384]{3,2,1,0:T(8,128)(2,1)}), bf16[4,4,144,384]{3,2,1,0:T(8,128)(2,1)S(1)}, u32[]{:S(2)}, u32[]{:S(2)}) async-start(bf16[4,4,144,384]{3,2,1,0:T(8,128)(2,1)} %get-tuple-element.8), calls=%async_computation | async-start | bytes 3538944 | tf_op jit(solution)/shard_map/all_to_all | solution.py:323
  51.3 1.0 concatenate.3
  52.3 1.6 constant_dynamic-slice_fusion.truth
  54.0 20.4 %all-to-all-done.fields = bf16[4,4,144,384]{3,2,1,0:T(8,128)(2,1)S(1)} async-done(((bf16[4,4,144,384]{3,2,1,0:T(8,128)(2,1)}), bf16[4,4,144,384]{3,2,1,0:T(8,128)(2,1)S(1)}, u32[]{:S(2)}, u32[]{:S(2)}) %all-to-all-start) | async-done | bytes 1769504 | tf_op jit(solution)/shard_map/all_to_all | solution.py:323
  74.3 0.8 broadcast_in_dim.25.rate
  75.2 0.7 broadcast_in_dim.27.scale
  75.9 10.7 %pairs.1 = bf16[4,4,144,384]{3,2,1,0:T(8,128)(2,1)} custom-call(bf16[4,4,144,384]{3,2,1,0:T(8,128)(2,1)} %copy-done, f32[144,384]{1,0:T(8,128)} %constant_dynamic-slice_fusion.truth, f32[144,128]{1,0:T(8,128)} %broadcast_in_dim.25.rate, f32[144,128]{1,0:T(8,128)} %broadcast_in_dim.27.scale), custom_call_target="tpu_custom_call" | custom-call | flops 56623104 | bytes 3538944 | tf_op jit(solution)/shard_map/pairs/pallas_call | solution.py:341
  86.6 33.1 %all_to_all.24.own = bf16[4,4,144,384]{3,2,1,0:T(8,128)(2,1)S(1)} all-to-all(bf16[4,4,144,384]{3,2,1,0:T(8,128)(2,1)} %pairs.1), channel_id=1, replica_groups=mesh['mem'=4,'lat'=8] {'mem'}, dimensions={0} | all-to-all | bytes 3538944 | tf_op jit(solution)/shard_map/all_to_all | solution.py:357
  119.8 54.3 %collective-permute-start.2 = (bf16[4,4,144,384]{3,2,1,0:T(8,128)(2,1)S(1)}, bf16[4,4,144,384]{3,2,1,0:T(8,128)(2,1)}, u32[]{:S(2)}, u32[]{:S(2)}) collective-permute-start(bf16[4,4,144,384]{3,2,1,0:T(8,128)(2,1)S(1)} %all_to_all.24.own), channel_id=1, source_target_pairs={{0,1},{1,2},{2,3},{3,4},{4,5},{5,6},{6,7},{8,9},{9,10},{10,11},{11... | collective-permute-start | bytes 5308424 | tf_op jit(solution)/shard_map/ppermute | solution.py:249
  174.0 1.3 collective-permute-start.3
  175.5 0.3 copy.18
  175.8 0.8 copy.31
  176.9 0.6 copy.19
  177.5 1.0 copy.29
  178.5 37.2 %collective-permute-done.3.bot = bf16[4,4,144,384]{3,2,1,0:T(8,128)(2,1)} collective-permute-done((bf16[4,4,144,384]{3,2,1,0:T(8,128)(2,1)S(1)}, bf16[4,4,144,384]{3,2,1,0:T(8,128)(2,1)}, u32[]{:S(2)}, u32[]{:S(2)}) %collective-permute-start.3) | collective-permute-done | bytes 1769504 | tf_op jit(solution)/shard_map/ppermute | solution.py:250
  215.8 39.3 %backward.1 = (bf16[4,2,1440,128]{3,2,1,0:T(8,128)(2,1)}, f32[1800,128]{1,0:T(8,128)}) custom-call(bf16[4,4,144,384]{3,2,1,0:T(8,128)(2,1)} %copy-done.1, bf16[4,4,144,384]{3,2,1,0:T(8,128)(2,1)} %collective-permute-done.2.top, bf16[4,4,144,384]{3,2,1,0:T(8,128)(2,1)} %collective-permute-done.3.bot, bf16[4,2,1536,128]{3,2,1,0:T(8,128)(2,1)} %get-tuple-element.9.hidden, ...), custom_call_target="tpu_custom_call" | custom-call | flops 22649241600 | bytes 25165824 | tf_op jit(solution)/shard_map/backward/pallas_call | solution.py:360
  255.1 1.2 convert.5
  256.4 50.0 %all_to_all.25 = bf16[32,64,128]{2,1,0:T(8,128)(2,1)S(1)} all-to-all(bf16[32,64,128]{2,1,0:T(8,128)(2,1)S(1)} %bitcast.61), channel_id=1, replica_groups=mesh['mem'=4,'lat'=8] {'mem','lat'}, dimensions={0} | all-to-all | bytes 1048576 | tf_op jit(solution)/shard_map/all_to_all | solution.py:259
  306.5 18.4 %all_to_all.26 = bf16[32,64,128]{2,1,0:T(8,128)(2,1)S(1)} all-to-all(bf16[32,64,128]{2,1,0:T(8,128)(2,1)S(1)} %broadcast_in_dim.28), channel_id=1, replica_groups=mesh['mem'=4,'lat'=8] {'mem','lat'}, dimensions={0} | all-to-all | bytes 1048576 | tf_op jit(solution)/shard_map/all_to_all | solution.py:262
  325.0 0.9 slice_multiply_fusion
  325.9 0.8 fusion
  (41 shorter events, 1.5 us)
Async XLA Ops:
  0.6 11.1 %collective-permute-start = (bf16[4,2,1440,128]{3,2,1,0:T(8,128)(2,1)}, bf16[4,2,1440,128]{3,2,1,0:T(8,128)(2,1)}, u32[]{:S(2)}, u32[]{:S(2)}) collective-permute-start(bf16[4,2,1440,128]{3,2,1,0:T(8,128)(2,1)} %feats.1), channel_id=1, source_target_pairs={{0,1},{1,2},{2,3},{3,4},{4,5},{5,6},{6,7},{8,9},{9,10},{10,11},{11... | collective-permute-start | bytes 8847368 | tf_op jit(solution)/shard_map/ppermute | solution.py:249
  4.6 8.1 %collective-permute-start.1 = (bf16[4,2,1440,128]{3,2,1,0:T(8,128)(2,1)}, bf16[4,2,1440,128]{3,2,1,0:T(8,128)(2,1)}, u32[]{:S(2)}, u32[]{:S(2)}) collective-permute-start(bf16[4,2,1440,128]{3,2,1,0:T(8,128)(2,1)} %feats.1), channel_id=1, source_target_pairs={{1,0},{2,1},{3,2},{4,3},{5,4},{6,5},{7,6},{9,8},{10,9},{11,10},{12... | collective-permute-start | bytes 8847368 | tf_op jit(solution)/shard_map/ppermute | solution.py:250
  6.9 2.2 copy-start.2
  45.4 5.3 %copy-start.3 = (f32[69,2,1440]{2,1,0:T(2,128)S(1)}, f32[69,2,1440]{2,1,0:T(2,128)}, u32[]{:S(2)}) copy-start(f32[69,2,1440]{2,1,0:T(2,128)} %param.9) | copy-start | bytes 2384644
  45.4 5.6 %copy-start.4 = (f32[69]{0:T(128)S(1)}, f32[69]{0:T(128)}, u32[]{:S(2)}) copy-start(f32[69]{0:T(128)} %param.11) | copy-start | bytes 832
  45.4 5.6 %copy-start.5 = (f32[69]{0:T(128)S(1)}, f32[69]{0:T(128)}, u32[]{:S(2)}) copy-start(f32[69]{0:T(128)} %param.10) | copy-start | bytes 832
  45.4 29.0 %all-to-all-start = ((bf16[4,4,144,384]{3,2,1,0:T(8,128)(2,1)}), bf16[4,4,144,384]{3,2,1,0:T(8,128)(2,1)S(1)}, u32[]{:S(2)}, u32[]{:S(2)}) async-start(bf16[4,4,144,384]{3,2,1,0:T(8,128)(2,1)} %get-tuple-element.8), calls=%async_computation | async-start | bytes 3538944 | tf_op jit(solution)/shard_map/all_to_all | solution.py:323
  74.3 1.6 copy-start
  119.7 57.1 %copy-start.1 = (bf16[4,4,144,384]{3,2,1,0:T(8,128)(2,1)}, bf16[4,4,144,384]{3,2,1,0:T(8,128)(2,1)S(1)}, u32[]{:S(2)}) copy-start(bf16[4,4,144,384]{3,2,1,0:T(8,128)(2,1)S(1)} %all_to_all.24.own) | copy-start | bytes 5308420
  119.8 58.8 %collective-permute-start.2 = (bf16[4,4,144,384]{3,2,1,0:T(8,128)(2,1)S(1)}, bf16[4,4,144,384]{3,2,1,0:T(8,128)(2,1)}, u32[]{:S(2)}, u32[]{:S(2)}) collective-permute-start(bf16[4,4,144,384]{3,2,1,0:T(8,128)(2,1)S(1)} %all_to_all.24.own), channel_id=1, source_target_pairs={{0,1},{1,2},{2,3},{3,4},{4,5},{5,6},{6,7},{8,9},{9,10},{10,11},{11... | collective-permute-start | bytes 5308424 | tf_op jit(solution)/shard_map/ppermute | solution.py:249
  174.0 41.7 %collective-permute-start.3 = (bf16[4,4,144,384]{3,2,1,0:T(8,128)(2,1)S(1)}, bf16[4,4,144,384]{3,2,1,0:T(8,128)(2,1)}, u32[]{:S(2)}, u32[]{:S(2)}) collective-permute-start(bf16[4,4,144,384]{3,2,1,0:T(8,128)(2,1)S(1)} %all_to_all.24.own), channel_id=1, source_target_pairs={{1,0},{2,1},{3,2},{4,3},{5,4},{6,5},{7,6},{9,8},{10,9},{11,10},{12... | collective-permute-start | bytes 5308424 | tf_op jit(solution)/shard_map/ppermute | solution.py:250

commit v2 on v1

v2 whole, which is shorter than its diff:
```python
import functools
import math

import jax
import jax.numpy as jnp
from jax import lax
from jax.experimental import pallas as pl
from jax.experimental.pallas import tpu as pltpu
from jax.sharding import PartitionSpec as P


BF16 = jnp.bfloat16
F32 = jnp.float32
LANES = 128
EDGE = 16
VMEM_LIMIT = 60 * 1024 * 1024
TILE = 480
AHEAD = 2
BACK = 2


def tile_of(count, step, most):
    return max(t for t in range(step, most + 1, step) if count % t == 0)


def wrap_edges(ref, lon):
    ref[0:EDGE] = ref[lon : lon + EDGE]
    ref[lon + EDGE : lon + 2 * EDGE] = ref[EDGE : 2 * EDGE]


def moved(values, offset, tile):
    if offset:
        values = pltpu.roll(values, (-offset) % values.shape[0], 0)
    return values[EDGE : EDGE + tile]


def three_taps(window, weights, offsets, tile):
    total = None
    for b, offset in enumerate(offsets):
        part = jnp.dot(window, weights[b], preferred_element_type=F32)
        part = moved(part, offset, tile)
        total = part if total is None else total + part
    return total


def forward_kernel(dims, flags, own, top, bot, w_inner, w_head, *refs):
    rows, lon, lon_pad, ch, qp, pieces, piece = dims
    hidden_out, slope_out, field_out, xs, hs, fs = refs[-6:]
    tile = tile_of(lon, 16, TILE)
    half = math.sqrt(2.0 / math.pi)
    for j in range(rows + 4):
        if j < 2:
            row = top[0, j]
        elif j < rows + 2:
            row = own[0, j - 2]
        else:
            row = bot[0, j - rows - 2]
        xs[EDGE : EDGE + lon, j * ch : (j + 1) * ch] = row
    wrap_edges(xs, lon)
    top_ok = flags[0].astype(F32)
    bot_ok = flags[1].astype(F32)

    def inner_step(t, carry):
        start = pl.multiple_of(t * tile, tile)
        for p in range((rows + 2) // 2):
            window = xs[pl.ds(start, tile + 2 * EDGE), 2 * p * ch : (2 * p + 4) * ch]
            pre = three_taps(window, w_inner, (-1, 0, 1), tile)
            square = pre * pre
            tanh = jnp.tanh(pre * (half + (half * 0.044715) * square))
            upper = 0.5 + 0.5 * tanh
            hidden = pre * upper
            slope = upper + hidden * (1.0 - upper) * (2.0 * half + (6.0 * half * 0.044715) * square)
            for k in range(2):
                i = 2 * p + k
                h = hidden[:, k * ch : (k + 1) * ch]
                s = slope[:, k * ch : (k + 1) * ch]
                if i == 0:
                    h, s = h * top_ok, s * top_ok
                if i == rows + 1:
                    h, s = h * bot_ok, s * bot_ok
                h = h.astype(BF16)
                hs[pl.ds(start + EDGE, tile), i * ch : (i + 1) * ch] = h
                slope_out[0, i, pl.ds(start, tile), :] = s.astype(BF16)
                if 1 <= i <= rows:
                    hidden_out[0, i - 1, pl.ds(start, tile), :] = h
        return carry

    lax.fori_loop(0, lon // tile, inner_step, 0)
    wrap_edges(hs, lon)
    zero = jnp.zeros((lon_pad - lon, ch), BF16)
    for i in range(rows + 2):
        slope_out[0, i, lon:lon_pad, :] = zero
    for i in range(rows):
        hidden_out[0, i, lon:lon_pad, :] = zero

    def head_step(t, carry):
        start = pl.multiple_of(t * tile, tile)
        for g in range(rows // 2):
            window = hs[pl.ds(start, tile + 2 * EDGE), 2 * g * ch : (2 * g + 4) * ch]
            fs[g, pl.ds(start, tile), :] = three_taps(window, w_head, (-1, 0, 1), tile)
        return carry

    lax.fori_loop(0, lon // tile, head_step, 0)
    pair = qp // (rows // 2)
    for g in range(rows // 2):
        fs[g, lon:lon_pad, :] = jnp.zeros((lon_pad - lon, fs.shape[2]), F32)
        fs[g, lon : lon + EDGE, :] = fs[g, 0:EDGE, :]
        fs[g, lon_pad - EDGE : lon_pad, :] = fs[g, lon - EDGE : lon, :]
        for j in range(pieces):
            turned = fs[g, j * piece : (j + 1) * piece, :].T
            field_out[j, 0, g * pair : (g + 1) * pair, :] = turned[:pair].astype(BF16)


def pair_kernel(dims, truth, rate, scale, *refs):
    members, taken, given, sub, piece = dims
    fields, outs, vals, accs = refs[:taken], refs[taken : taken + given], refs[-2], refs[-1]
    norm = 2.0 / (members - 1)
    pieces = fields[0].shape[0]
    for j in range(pieces):
        m = j * (members // pieces)
        for ref in fields:
            for k in range(ref.shape[1]):
                vals[m] = ref[j, k].astype(F32)
                m += 1
    blocks = piece // LANES

    def step(t, carry):
        r = pl.ds(pl.multiple_of((t // blocks) * 8, 8), 8)
        c = pl.ds(pl.multiple_of((t % blocks) * LANES, LANES), LANES)
        neg = rate[r, :]
        x = [vals[m, r, c] for m in range(members)]
        sums = [None] * members
        for i in range(members):
            for j in range(i + 1, members):
                d = x[j] - x[i]
                w = jnp.exp2(d * d * neg) * d
                sums[i] = w if sums[i] is None else sums[i] + w
                sums[j] = -w if sums[j] is None else sums[j] - w
        y = truth[r, c]
        sc = scale[r, :]
        for i in range(members):
            off = x[i] - y
            near = jnp.exp2(off * off * neg) * off
            accs[i, r, c] = sc * (norm * sums[i] + 2.0 * near)
        return carry

    lax.fori_loop(0, (sub // 8) * blocks, step, 0)
    for j in range(pieces):
        m = j * (members // pieces)
        for ref in outs:
            for k in range(ref.shape[1]):
                ref[j, k] = accs[m].astype(BF16)
                m += 1


def backward_kernel(dims, own, top, bot, hidden, slope, feats, w_back, *refs):
    rows, lon, lon_pad, ch, vp, pieces, piece, low, span = dims
    back_out, sums_out, gs, fx, acc_in, acc_hd = refs[-6:]
    ext = (rows + 4) * vp
    step_m = pl.program_id(0)

    @pl.when(step_m == 0)
    def _():
        acc_in[...] = jnp.zeros_like(acc_in)
        acc_hd[...] = jnp.zeros_like(acc_hd)

    for j in range(pieces):
        cols = slice(j * piece, (j + 1) * piece)
        gs[1, 0 : 2 * vp, cols] = top[j, 0]
        gs[1, 2 * vp : ext - 2 * vp, cols] = own[j, 0]
        gs[1, ext - 2 * vp : ext, cols] = bot[j, 0]
    for t in range(ext // 16):
        r = slice(t * 16, (t + 1) * 16)
        block = gs[1, r, :].astype(F32)
        gs[0, r, :] = pltpu.roll(block, lon_pad - 1, 1).astype(BF16)
        gs[2, r, :] = pltpu.roll(block, 1, 1).astype(BF16)
    for r in range(rows):
        fx[EDGE : EDGE + lon, r * ch : (r + 1) * ch] = feats[0, r]
    wrap_edges(fx, lon)
    fx[lon + 2 * EDGE :] = jnp.zeros((lon_pad - lon, rows * ch), BF16)
    tile = tile_of(lon_pad, LANES, 512)

    def step(t, carry):
        start = pl.multiple_of(t * tile, tile)
        rows_back = []
        for p in range((rows + 2) // 2):
            patch = jnp.concatenate(
                [gs[b, 2 * p * vp : (2 * p + 4) * vp, pl.ds(start, tile)] for b in range(3)], axis=0
            )
            back = lax.dot_general(
                patch, w_back[...], (((0,), (0,)), ((), ())), preferred_element_type=F32
            )
            for k in range(2):
                i = 2 * p + k
                part = back[:, k * ch : (k + 1) * ch] * slope[0, i, pl.ds(start, tile), :].astype(F32)
                part = part.astype(BF16)
                back_out[0, i, pl.ds(start, tile), :] = part
                rows_back.append(part)
        for g in range(rows // 2):
            base = 2 * g * vp + low
            patch = jnp.concatenate(
                [gs[b, base : base + span, pl.ds(start, tile)] for b in range(3)], axis=0
            )
            act = jnp.concatenate(
                [hidden[0, 2 * g + k, pl.ds(start, tile), :] for k in range(2)], axis=1
            )
            acc_hd[...] += jnp.dot(patch, act, preferred_element_type=F32)
            window = fx[pl.ds(start, tile + 2 * EDGE), 2 * g * ch : (2 * g + 2) * ch].astype(F32)
            act = jnp.concatenate(
                [moved(window, off, tile).astype(BF16) for off in (-1, 0, 1)], axis=1
            )
            back = jnp.concatenate(rows_back[2 * g : 2 * g + 4], axis=1)
            acc_in[...] += lax.dot_general(
                act, back, (((0,), (0,)), ((), ())), preferred_element_type=F32
            )
        return carry

    lax.fori_loop(0, lon_pad // tile, step, 0)

    @pl.when(step_m == pl.num_programs(0) - 1)
    def _():
        for a in range(3):
            for b in range(3):
                inner = None
                head = None
                for k in range(2):
                    n = k + 2 - a
                    at = b * 2 * ch + k * ch
                    part = acc_in[at : at + ch, n * ch : (n + 1) * ch]
                    inner = part if inner is None else inner + part
                    n = k + 3 - a
                    at = b * span + n * vp - low
                    part = acc_hd[at : at + vp, k * ch : (k + 1) * ch]
                    head = part if head is None else head + part
                q = 3 * a + b
                sums_out[q * ch : (q + 1) * ch, :] = inner
                at = 9 * ch + q * vp
                sums_out[at : at + vp, :] = head


def feature_kernel(dims, back, w_grad, grad_out, bs):
    rows, lon, ch = dims
    for i in range(rows + 2):
        bs[EDGE : EDGE + lon, i * ch : (i + 1) * ch] = back[0, i, :lon]
    wrap_edges(bs, lon)
    tile = tile_of(lon, 16, TILE)

    def step(t, carry):
        start = pl.multiple_of(t * tile, tile)
        for g in range(rows // 2):
            window = bs[pl.ds(start, tile + 2 * EDGE), 2 * g * ch : (2 * g + 4) * ch]
            grad = three_taps(window, w_grad, (1, 0, -1), tile)
            for k in range(2):
                grad_out[0, 2 * g + k, pl.ds(start, tile), :] = grad[
                    :, k * ch : (k + 1) * ch
                ].astype(BF16)
        return carry

    lax.fori_loop(0, lon // tile, step, 0)


def forward_weights(kernel, width):
    ch, outs = kernel.shape[2], kernel.shape[3]
    kernel = jnp.pad(kernel, ((0, 0), (0, 0), (0, 0), (0, width - outs)))
    cols = []
    for out_row in range(2):
        taps = jnp.pad(kernel, ((out_row, 1 - out_row), (0, 0), (0, 0), (0, 0)))
        cols.append(jnp.moveaxis(taps, 0, 1))
    return jnp.stack(cols, axis=3).reshape(3, 4 * ch, 2 * width)


def backward_weights(kernel, width):
    ch, outs = kernel.shape[2], kernel.shape[3]
    kernel = jnp.pad(kernel, ((0, 0), (0, 0), (0, 0), (0, width - outs)))[::-1]
    cols = []
    for out_row in range(2):
        taps = jnp.pad(kernel, ((out_row, 1 - out_row), (0, 0), (0, 0), (0, 0)))
        cols.append(jnp.transpose(taps, (1, 0, 3, 2)))
    return jnp.stack(cols, axis=3).reshape(3, 4 * width, 2 * ch)


def groups_of(count, groups):
    out, first = [], 0
    for g in range(min(groups, count)):
        size = -(-(count - first) // (min(groups, count) - g))
        out.append((first, size))
        first += size
    return out


def neighbours(tail, head, axis):
    count = lax.axis_size(axis)
    before = lax.ppermute(tail, axis, [(i, i + 1) for i in range(count - 1)])
    after = lax.ppermute(head, axis, [(i + 1, i) for i in range(count - 1)])
    return before, after


def reduce_all(values, axes):
    count = math.prod(lax.axis_size(a) for a in axes)
    rows, width = values.shape
    part = -(-rows // (16 * count)) * 16
    padded = jnp.pad(values, ((0, part * count - rows), (0, 0))).astype(BF16)
    got = lax.all_to_all(padded, axes, 0, 0, tiled=True)
    summed = jnp.sum(got.reshape(count, part, width).astype(F32), axis=0).astype(BF16)
    spread = jnp.broadcast_to(summed[None], (count, part, width))
    full = lax.all_to_all(spread, axes, 0, 0)
    return full.reshape(count * part, width)[:rows].astype(F32)


def shards(features, conv_inner, conv_head, truth, kernel_width, var_weight):
    per, rows, lon, ch = features.shape
    variables = conv_head.shape[3]
    pieces = lax.axis_size("mem")
    members = per * pieces
    vp = -(-variables // 8) * 8
    qp = rows * vp
    piece = -(-lon // (LANES * pieces)) * LANES
    while lon + 2 * EDGE > piece * pieces:
        piece += LANES
    lon_pad = piece * pieces
    assert rows % 2 == 0 and lon % 16 == 0 and (2 * vp) % 16 == 0 and 2 * vp <= 256
    low = vp // 16 * 16
    span = -(-(5 * vp - low) // 16) * 16

    at = lax.axis_index("lat")
    flags = jnp.stack([at > 0, at < lax.axis_size("lat") - 1]).astype(jnp.int32)

    w_inner = forward_weights(conv_inner, ch)
    w_head = jnp.pad(forward_weights(conv_head, vp), ((0, 0), (0, 0), (0, 256 - 2 * vp)))
    w_back = backward_weights(conv_head, vp).reshape(12 * vp, 2 * ch)
    w_grad = backward_weights(conv_inner, ch)

    params = functools.partial(pltpu.CompilerParams, vmem_limit_bytes=VMEM_LIMIT)
    whole = lambda shape: pl.BlockSpec(shape, lambda m: (0,) * len(shape))
    member = lambda shape, base=0: pl.BlockSpec((1,) + shape, lambda m: (base + m,) + (0,) * len(shape))
    spread = lambda n: pl.BlockSpec((pieces, 1, n, piece), lambda m: (0, m, 0, 0))
    macs = 2 * lon * 12 * ch * 2 * ch

    kept_shapes = [
        jax.ShapeDtypeStruct((per, rows, lon_pad, ch), BF16),
        jax.ShapeDtypeStruct((per, rows + 2, lon_pad, ch), BF16),
    ]
    ahead, behind = groups_of(per, AHEAD), groups_of(per, BACK)

    def forward(first, count, kept):
        mine = features[first : first + count]
        top, bot = neighbours(mine[:, rows - 2 :], mine[:, :2], "lat")
        return pl.pallas_call(
            functools.partial(forward_kernel, (rows, lon, lon_pad, ch, qp, pieces, piece)),
            grid=(count,),
            in_specs=[
                pl.BlockSpec(memory_space=pltpu.SMEM),
                member((rows, lon, ch), first),
                member((2, lon, ch)),
                member((2, lon, ch)),
                whole(w_inner.shape),
                whole(w_head.shape),
            ]
            + [pl.BlockSpec(memory_space=pl.ANY)] * len(kept),
            out_specs=[
                member((rows, lon_pad, ch), first),
                member((rows + 2, lon_pad, ch), first),
                spread(qp),
            ],
            out_shape=kept_shapes + [jax.ShapeDtypeStruct((pieces, count, qp, piece), BF16)],
            input_output_aliases={6 + k: k for k in range(len(kept))},
            scratch_shapes=[
                pltpu.VMEM((lon + 2 * EDGE, (rows + 4) * ch), BF16),
                pltpu.VMEM((lon + 2 * EDGE, (rows + 2) * ch), BF16),
                pltpu.VMEM((rows // 2, lon_pad, 256), F32),
            ],
            compiler_params=params(),
            cost_estimate=pl.CostEstimate(
                flops=3 * macs * count, bytes_accessed=(6 << 20) * count, transcendentals=0
            ),
            name="forward",
        )(flags, features, top, bot, w_inner, w_head, *kept)

    kept, traded = [], []
    for first, count in ahead:
        *kept, field = forward(first, count, kept)
        traded.append(lax.all_to_all(field, "mem", 0, 0, tiled=True))

    truth_rows = jnp.moveaxis(truth, 1, 0)
    truth_rows = jnp.pad(truth_rows, ((0, 0), (0, vp - variables), (0, 0))).reshape(qp, lon)
    middle = jnp.zeros((qp, lon_pad - lon - 2 * EDGE), F32)
    truth_rows = jnp.concatenate(
        [truth_rows, truth_rows[:, :EDGE], middle, truth_rows[:, lon - EDGE :]], axis=1
    )
    truth_piece = lax.dynamic_slice_in_dim(truth_rows, lax.axis_index("mem") * piece, piece, 1)
    inverse = 1.0 / (kernel_width * kernel_width)
    spread_param = lambda v: jnp.broadcast_to(
        jnp.tile(jnp.pad(v, (0, vp - variables)), rows)[:, None], (qp, LANES)
    )
    rate = spread_param((-0.5 * math.log2(math.e)) * inverse)
    scale = spread_param(var_weight * inverse)
    sub = 16
    row_block = lambda width: pl.BlockSpec((sub, width), lambda i: (i, 0))
    field_block = lambda count: pl.BlockSpec((pieces, count, sub, piece), lambda i: (0, 0, i, 0))
    gradient = pl.pallas_call(
        functools.partial(pair_kernel, (members, len(ahead), len(behind), sub, piece)),
        grid=(qp // sub,),
        in_specs=[row_block(piece), row_block(LANES), row_block(LANES)]
        + [field_block(count) for _, count in ahead],
        out_specs=[field_block(count) for _, count in behind],
        out_shape=[
            jax.ShapeDtypeStruct((pieces, count, qp, piece), BF16) for _, count in behind
        ],
        scratch_shapes=[pltpu.VMEM((members, sub, piece), F32)] * 2,
        compiler_params=params(),
        cost_estimate=pl.CostEstimate(
            flops=4 * members * members * qp * piece,
            bytes_accessed=4 * members * qp * piece,
            transcendentals=members * members // 2 * qp * piece,
        ),
        name="pairs",
    )(truth_piece, rate, scale, *traded)

    sums_rows = 9 * (ch + vp)

    def backward(own, first, count, back):
        g_top, g_bot = neighbours(own[:, :, qp - 2 * vp :], own[:, :, : 2 * vp], "lat")
        return pl.pallas_call(
            functools.partial(
                backward_kernel, (rows, lon, lon_pad, ch, vp, pieces, piece, low, span)
            ),
            grid=(count,),
            in_specs=[
                spread(qp),
                spread(2 * vp),
                spread(2 * vp),
                member((rows, lon_pad, ch), first),
                member((rows + 2, lon_pad, ch), first),
                member((rows, lon, ch), first),
                whole(w_back.shape),
            ]
            + [pl.BlockSpec(memory_space=pl.ANY)] * len(back),
            out_specs=[member((rows + 2, lon_pad, ch), first), whole((sums_rows, ch))],
            out_shape=[kept_shapes[1], jax.ShapeDtypeStruct((sums_rows, ch), F32)],
            input_output_aliases={7 + k: k for k in range(len(back))},
            scratch_shapes=[
                pltpu.VMEM((3, (rows + 4) * vp, lon_pad), BF16),
                pltpu.VMEM((lon_pad + 2 * EDGE, rows * ch), BF16),
                pltpu.VMEM((6 * ch, 4 * ch), F32),
                pltpu.VMEM((3 * span, 2 * ch), F32),
            ],
            compiler_params=params(),
            cost_estimate=pl.CostEstimate(
                flops=4 * macs * count, bytes_accessed=(6 << 20) * count, transcendentals=0
            ),
            name="backward",
        )(own, g_top, g_bot, *kept, features, w_back, *back)

    owned, back, sums = [], [], None
    for g in gradient:
        owned.append(lax.all_to_all(g, "mem", 0, 0, tiled=True))
    for own, chunk in zip(owned, behind):
        *back, part = backward(own, *chunk, back)
        sums = part if sums is None else sums + part
    grad_features = pl.pallas_call(
        functools.partial(feature_kernel, (rows, lon, ch)),
        grid=(per,),
        in_specs=[member((rows + 2, lon_pad, ch)), whole(w_grad.shape)],
        out_specs=member((rows, lon, ch)),
        out_shape=jax.ShapeDtypeStruct(features.shape, BF16),
        scratch_shapes=[pltpu.VMEM((lon + 2 * EDGE, (rows + 2) * ch), BF16)],
        compiler_params=params(),
        cost_estimate=pl.CostEstimate(
            flops=macs * per, bytes_accessed=(4 << 20) * per, transcendentals=0
        ),
        name="features",
    )(*back, w_grad)

    total = reduce_all(sums, ("mem", "lat"))
    points = rows * lax.axis_size("lat") * lon
    inner_sum = total[: 9 * ch].reshape(3, 3, ch, ch)
    head_sum = total[9 * ch :].reshape(3, 3, vp, ch)[:, :, :variables]
    return (grad_features, inner_sum / points, jnp.swapaxes(head_sum, 2, 3) / points)


def solution(mesh):
    in_specs = (P("mem", "lat", None, None), P(), P(), P(None, "lat", None), P(), P())
    out_specs = (P("mem", "lat", None, None), P(), P())

    return jax.shard_map(shards, mesh=mesh, in_specs=in_specs, out_specs=out_specs, check_vma=False)
```

time: 327 us -> 286 us (0.87)
  waiting for transfers between devices: 58.6 us -> 18.8 us
  blocking collectives: 102 us -> 76.5 us
  starting transfers between devices: 66.1 us -> 85.7 us
    ppermute x2 -> x4, waiting for transfers between devices: 38.3 us -> 3.19 us  [neighbours(): after = lax.ppermute(head, axis, [(i + 1, i) for i in range(count - 1)])]
    all_to_all x1, blocking collectives: 50 us -> 32.3 us  [reduce_all(): got = lax.all_to_all(padded, axes, 0, 0, tiled=True)]
    ppermute x2 -> x4, starting transfers between devices: 58.3 us -> 69.5 us  [neighbours(): before = lax.ppermute(tail, axis, [(i, i + 1) for i in range(count - 1)])]
    all_to_all x2, blocking collectives: 51.5 us -> 44.1 us  [the longest x1 24.9 us: shards(): owned.append(lax.all_to_all(g, 'mem', 0, 0, tiled=True))]
    all_to_all x1 -> x3, starting transfers between devices: 5.32 us -> 10.8 us  [the longest x1 4.34 us: shards(): traded.append(lax.all_to_all(field, 'mem', 0, 0, tiled=True))]
    all_to_all x1 -> x3, waiting for transfers between devices: 20.4 us -> 15.6 us  [the longest x1 12.7 us: shards(): traded.append(lax.all_to_all(field, 'mem', 0, 0, tiled=True))]
    pallas_call x3 -> x6, Pallas kernels: 82.6 us -> 84.4 us  [the longest x2 33.8 us: forward(): pl.pallas_call(functools.partial(forward_kernel, (rows, lon, lon_pad, ch,...]
  transfers between devices with their start and end apart: 5 -> 11, of which waited for: 3 -> 3; matrix products, arithmetic and copies ran while one was open for 4% -> 4% of each run, Pallas kernels for 0% -> 15%
where the time goes in v2:
time: 286 us; the launch traced here: 285 us
  starting transfers between devices  85.7 us (30%)
  Pallas kernels  84.4 us (30%)
  blocking collectives  76.5 us (27%)
  waiting for transfers between devices  18.8 us (7%)
  local copies, waits for them, and re-layouts  14.9 us (5%)
  other arithmetic  3.99 us (1%)
    ppermute x4, starting transfers between devices, neighbours(): before = lax.ppermute(tail, axis, [(i, i + 1) for i in range(count - 1)])  69.5 us
    pallas_call x2, Pallas kernels, forward(): pl.pallas_call(functools.partial(forward_kernel, (rows, lon, lon_pad, ch,...  33.8 us
    all_to_all x1, blocking collectives, reduce_all(): got = lax.all_to_all(padded, axes, 0, 0, tiled=True)  32.3 us
    pallas_call x2, Pallas kernels, backward(): pl.pallas_call(functools.partial(backward_kernel, (rows, lon, lon_pad, ch...  29.3 us
    all_to_all x1, blocking collectives, shards(): owned.append(lax.all_to_all(g, 'mem', 0, 0, tiled=True))  24.9 us
    all_to_all x1, blocking collectives, shards(): traded.append(lax.all_to_all(field, 'mem', 0, 0, tiled=True))  19.2 us
    all_to_all x1, waiting for transfers between devices, shards(): traded.append(lax.all_to_all(field, 'mem', 0, 0, tiled=True))  12.7 us
    pallas_call x1, Pallas kernels, shards(): pl.pallas_call(functools.partial(pair_kernel, (members, len(ahead), len(b...  10.9 us
  transfers between devices with their start and end apart: 11, of which 3 were waited for; matrix products, arithmetic and copies ran while one was open for 4% of the time, Pallas kernels for 15%

profile of v2, /device:TPU:0, one launch (start us, length us, event | category | flops | bytes accessed | tf_op | source)
XLA Modules:
  0.0 285.3 jit_solution(13588457829039032031)
XLA Ops:
  0.6 3.2 %fusion.2 = (bf16[2,2,1440,128]{3,2,1,0:T(8,128)(2,1)S(1)}, bf16[2,2,1440,128]{3,2,1,0:T(8,128)(2,1)}) fusion(bf16[4,2,1440,128]{3,2,1,0:T(8,128)(2,1)} %feats.3), kind=kLoop, calls=%fused_computation.23 | loop fusion | bytes 5898240 | tf_op jit(solution)/shard_map/slice | solution.py:346
  3.8 3.5 %collective-permute-start = (bf16[2,2,1440,128]{3,2,1,0:T(8,128)(2,1)}, bf16[2,2,1440,128]{3,2,1,0:T(8,128)(2,1)}, u32[]{:S(2)}, u32[]{:S(2)}) collective-permute-start(bf16[2,2,1440,128]{3,2,1,0:T(8,128)(2,1)} %get-tuple-element.30), channel_id=1, source_target_pairs={{0,1},{1,2},{2,3},{3,4},{4,5},{5,6},{6,7},{8,9},{9,10},{10,11},{11... | collective-permute-start | bytes 4423688 | tf_op jit(solution)/shard_map/ppermute | solution.py:293
  7.3 1.3 collective-permute-start.1
  8.6 5.2 %collective-permute-start.2 = (bf16[2,2,1440,128]{3,2,1,0:T(8,128)(2,1)S(1)}, bf16[2,2,1440,128]{3,2,1,0:T(8,128)(2,1)}, u32[]{:S(2)}, u32[]{:S(2)}) collective-permute-start(bf16[2,2,1440,128]{3,2,1,0:T(8,128)(2,1)S(1)} %get-tuple-element.29), channel_id=1, source_target_pairs={{0,1},{1,2},{2,3},{3,4},{4,5},{5,6},{6,7},{8,9},{9,10},{10,11},{11... | collective-permute-start | bytes 4423688 | tf_op jit(solution)/shard_map/ppermute | solution.py:293
  13.8 1.3 collective-permute-start.3
  16.3 1.0 pad.61.w_head
  17.6 0.8 copy.18
  18.4 1.5 reshape.37.w_inner
  20.5 16.9 %forward.2 = (bf16[4,2,1536,128]{3,2,1,0:T(8,128)(2,1)}, bf16[4,4,1536,128]{3,2,1,0:T(8,128)(2,1)}, bf16[4,2,144,384]{3,2,1,0:T(8,128)(2,1)}) custom-call(s32[2]{0:T(128)} %add_convert_fusion.1.flags, bf16[4,2,1440,128]{3,2,1,0:T(8,128)(2,1)} %feats.3, bf16[2,2,1440,128]{3,2,1,0:T(8,128)(2,1)} %collective-permute-done.top, ...), custom_call_target="tpu_custom_call" | custom-call | flops 6794772480 | bytes 12582912 | tf_op jit(solution)/shard_map/forward/pallas_call | solution.py:348
  37.4 16.9 %forward.3 = (bf16[4,2,1536,128]{3,2,1,0:T(8,128)(2,1)}, bf16[4,4,1536,128]{3,2,1,0:T(8,128)(2,1)}, bf16[4,2,144,384]{3,2,1,0:T(8,128)(2,1)}) custom-call(s32[2]{0:T(128)} %add_convert_fusion.1.flags, bf16[4,2,1440,128]{3,2,1,0:T(8,128)(2,1)} %feats.3, ...), custom_call_target="tpu_custom_call", output_to_operand_aliasing={{0}: (6, {}), {1}: (7, {})} | custom-call | flops 6794772480 | bytes 12582912 | tf_op jit(solution)/shard_map/forward/pallas_call | solution.py:348
  54.3 19.2 %all_to_all.34.refs_1_ = bf16[4,2,144,384]{3,2,1,0:T(8,128)(2,1)} all-to-all(bf16[4,2,144,384]{3,2,1,0:T(8,128)(2,1)} %get-tuple-element.18), channel_id=1, replica_groups=mesh['mem'=4,'lat'=8] {'mem'}, dimensions={0} | all-to-all | bytes 1769472 | tf_op jit(solution)/shard_map/all_to_all | solution.py:382
  73.5 4.3 %all-to-all-start = ((bf16[4,2,144,384]{3,2,1,0:T(8,128)(2,1)}), bf16[4,2,144,384]{3,2,1,0:T(8,128)(2,1)}, u32[]{:S(2)}, u32[]{:S(2)}) async-start(bf16[4,2,144,384]{3,2,1,0:T(8,128)(2,1)} %get-tuple-element.15), calls=%async_computation | async-start | bytes 1769472 | tf_op jit(solution)/shard_map/all_to_all | solution.py:382
  79.3 12.7 %all-to-all-done.refs_0_ = bf16[4,2,144,384]{3,2,1,0:T(8,128)(2,1)} async-done(((bf16[4,2,144,384]{3,2,1,0:T(8,128)(2,1)}), bf16[4,2,144,384]{3,2,1,0:T(8,128)(2,1)}, u32[]{:S(2)}, u32[]{:S(2)}) %all-to-all-start) | async-done | bytes 884768 | tf_op jit(solution)/shard_map/all_to_all | solution.py:382
  93.5 10.9 %pairs.1 = (bf16[4,2,144,384]{3,2,1,0:T(8,128)(2,1)}, bf16[4,2,144,384]{3,2,1,0:T(8,128)(2,1)}) custom-call(f32[144,384]{1,0:T(8,128)} %constant_dynamic-slice_fusion.truth, f32[144,128]{1,0:T(8,128)} %broadcast_in_dim.25.rate, f32[144,128]{1,0:T(8,128)} %broadcast_in_dim.27.scale, bf16[4,2,144,384]{3,2,1,0:T(8,128)(2,1)} %all-to-all-done.refs_0_, ...), custom_call_target="tpu_custom_call" | custom-call | flops 56623104 | bytes 3538944 | tf_op jit(solution)/shard_map/pairs/pallas_call | solution.py:400
  104.4 24.9 %all_to_all.35.own = bf16[4,2,144,384]{3,2,1,0:T(8,128)(2,1)S(1)} all-to-all(bf16[4,2,144,384]{3,2,1,0:T(8,128)(2,1)} %get-tuple-element.22), channel_id=1, replica_groups=mesh['mem'=4,'lat'=8] {'mem'}, dimensions={0} | all-to-all | bytes 1769472 | tf_op jit(solution)/shard_map/all_to_all | solution.py:456
  129.3 3.5 %all-to-all-start.2 = ((bf16[4,2,144,384]{3,2,1,0:T(8,128)(2,1)}), bf16[4,2,144,384]{3,2,1,0:T(8,128)(2,1)S(1)}, u32[]{:S(2)}, u32[]{:S(2)}) async-start(bf16[4,2,144,384]{3,2,1,0:T(8,128)(2,1)} %get-tuple-element.19), calls=%async_computation.2 | async-start | bytes 1769472 | tf_op jit(solution)/shard_map/all_to_all | solution.py:456
  132.8 33.8 %collective-permute-start.6 = (bf16[4,2,144,384]{3,2,1,0:T(8,128)(2,1)S(1)}, bf16[4,2,144,384]{3,2,1,0:T(8,128)(2,1)}, u32[]{:S(2)}, u32[]{:S(2)}) collective-permute-start(bf16[4,2,144,384]{3,2,1,0:T(8,128)(2,1)S(1)} %all_to_all.35.own), channel_id=1, source_target_pairs={{0,1},{1,2},{2,3},{3,4},{4,5},{5,6},{6,7},{8,9},{9,10},{10,11},{11... | collective-permute-start | bytes 2654216 | tf_op jit(solution)/shard_map/ppermute | solution.py:293
  166.6 1.3 collective-permute-start.7
  168.0 27.1 %collective-permute-start.4 = (bf16[4,2,144,384]{3,2,1,0:T(8,128)(2,1)S(1)}, bf16[4,2,144,384]{3,2,1,0:T(8,128)(2,1)}, u32[]{:S(2)}, u32[]{:S(2)}) collective-permute-start(bf16[4,2,144,384]{3,2,1,0:T(8,128)(2,1)S(1)} %all-to-all-done.2.own), channel_id=1, source_target_pairs={{0,1},{1,2},{2,3},{3,4},{4,5},{5,6},{6,7},{8,9},{9,10},{10,11},{11... | collective-permute-start | bytes 2654216 | tf_op jit(solution)/shard_map/ppermute | solution.py:293
  195.1 1.5 collective-permute-start.5
  196.9 0.8 copy.28
  197.8 14.6 %backward.2 = (bf16[4,4,1536,128]{3,2,1,0:T(8,128)(2,1)}, f32[1800,128]{1,0:T(8,128)}) custom-call(bf16[4,2,144,384]{3,2,1,0:T(8,128)(2,1)} %copy-done.3, bf16[4,2,144,384]{3,2,1,0:T(8,128)(2,1)} %collective-permute-done.6.top, bf16[4,2,144,384]{3,2,1,0:T(8,128)(2,1)} %collective-permute-done.7.bot, bf16[4,2,1536,128]{3,2,1,0:T(8,128)(2,1)} %get-tuple-element.20.hidden, ...), custom_call_target="tpu_custom_call" | custom-call | flops 9059696640 | bytes 12582912 | tf_op jit(solution)/shard_map/backward/pallas_call | solution.py:423
  212.4 3.2 %collective-permute-done.5.bot = bf16[4,2,144,384]{3,2,1,0:T(8,128)(2,1)} collective-permute-done((bf16[4,2,144,384]{3,2,1,0:T(8,128)(2,1)S(1)}, bf16[4,2,144,384]{3,2,1,0:T(8,128)(2,1)}, u32[]{:S(2)}, u32[]{:S(2)}) %collective-permute-start.5) | collective-permute-done | bytes 884768 | tf_op jit(solution)/shard_map/ppermute | solution.py:294
  215.6 14.7 %backward.3 = (bf16[4,4,1536,128]{3,2,1,0:T(8,128)(2,1)}, f32[1800,128]{1,0:T(8,128)}) custom-call(bf16[4,2,144,384]{3,2,1,0:T(8,128)(2,1)} %copy-done.2, bf16[4,2,144,384]{3,2,1,0:T(8,128)(2,1)} %collective-permute-done.4.top, bf16[4,2,144,384]{3,2,1,0:T(8,128)(2,1)} %collective-permute-done.5.bot, ...), custom_call_target="tpu_custom_call", output_to_operand_aliasing={{0}: (7, {})} | custom-call | flops 9059696640 | bytes 12582912 | tf_op jit(solution)/shard_map/backward/pallas_call | solution.py:423
  230.3 1.3 add_convert_fusion
  231.7 32.3 %all_to_all.36 = bf16[32,64,128]{2,1,0:T(8,128)(2,1)S(1)} all-to-all(bf16[32,64,128]{2,1,0:T(8,128)(2,1)S(1)} %bitcast.49), channel_id=1, replica_groups=mesh['mem'=4,'lat'=8] {'mem','lat'}, dimensions={0} | all-to-all | bytes 1048576 | tf_op jit(solution)/shard_map/all_to_all | solution.py:303
  264.1 0.9 broadcast_in_dim.28
  265.0 3.0 %all-to-all-start.5 = ((bf16[32,64,128]{2,1,0:T(8,128)(2,1)}), bf16[32,64,128]{2,1,0:T(8,128)(2,1)S(1)}, u32[]{:S(2)}, u32[]{:S(2)}) async-start(bf16[32,64,128]{2,1,0:T(8,128)(2,1)} %broadcast_in_dim.28), calls=%async_computation.5 | async-start | bytes 1048576 | tf_op jit(solution)/shard_map/all_to_all | solution.py:306
  268.8 1.4 reshape.39.w_grad
  270.2 10.5 %features.1 = bf16[4,2,1440,128]{3,2,1,0:T(8,128)(2,1)} custom-call(bf16[4,4,1536,128]{3,2,1,0:T(8,128)(2,1)} %get-tuple-element.24.back, bf16[3,512,256]{2,1,0:T(8,128)(2,1)} %reshape.39.w_grad), custom_call_target="tpu_custom_call" | custom-call | flops 4529848320 | bytes 16777216 | tf_op jit(solution)/shard_map/features/pallas_call | solution.py:460
  280.7 2.9 %all-to-all-done.5 = bf16[32,64,128]{2,1,0:T(8,128)(2,1)S(1)} async-done(((bf16[32,64,128]{2,1,0:T(8,128)(2,1)}), bf16[32,64,128]{2,1,0:T(8,128)(2,1)S(1)}, u32[]{:S(2)}, u32[]{:S(2)}) %all-to-all-start.5) | async-done | bytes 524320 | tf_op jit(solution)/shard_map/all_to_all | solution.py:306
  283.7 0.9 slice_multiply_fusion
  (61 shorter events, 7.1 us)
Async XLA Ops:
  0.6 14.4 %copy-start.5 = (bf16[3,3,128,69]{2,3,1,0:T(8,128)(2,1)S(1)}, bf16[3,3,128,69]{2,3,1,0:T(8,128)(2,1)}, u32[]{:S(2)}) copy-start(bf16[3,3,128,69]{2,3,1,0:T(8,128)(2,1)} %param.8) | copy-start | bytes 476932
  3.8 16.7 %collective-permute-start = (bf16[2,2,1440,128]{3,2,1,0:T(8,128)(2,1)}, bf16[2,2,1440,128]{3,2,1,0:T(8,128)(2,1)}, u32[]{:S(2)}, u32[]{:S(2)}) collective-permute-start(bf16[2,2,1440,128]{3,2,1,0:T(8,128)(2,1)} %get-tuple-element.30), channel_id=1, source_target_pairs={{0,1},{1,2},{2,3},{3,4},{4,5},{5,6},{6,7},{8,9},{9,10},{10,11},{11... | collective-permute-start | bytes 4423688 | tf_op jit(solution)/shard_map/ppermute | solution.py:293
  7.3 13.2 %collective-permute-start.1 = (bf16[2,2,1440,128]{3,2,1,0:T(8,128)(2,1)}, bf16[2,2,1440,128]{3,2,1,0:T(8,128)(2,1)}, u32[]{:S(2)}, u32[]{:S(2)}) collective-permute-start(bf16[2,2,1440,128]{3,2,1,0:T(8,128)(2,1)} %get-tuple-element.30), channel_id=1, source_target_pairs={{1,0},{2,1},{3,2},{4,3},{5,4},{6,5},{7,6},{9,8},{10,9},{11,10},{12... | collective-permute-start | bytes 4423688 | tf_op jit(solution)/shard_map/ppermute | solution.py:294
  8.6 28.7 %collective-permute-start.2 = (bf16[2,2,1440,128]{3,2,1,0:T(8,128)(2,1)S(1)}, bf16[2,2,1440,128]{3,2,1,0:T(8,128)(2,1)}, u32[]{:S(2)}, u32[]{:S(2)}) collective-permute-start(bf16[2,2,1440,128]{3,2,1,0:T(8,128)(2,1)S(1)} %get-tuple-element.29), channel_id=1, source_target_pairs={{0,1},{1,2},{2,3},{3,4},{4,5},{5,6},{6,7},{8,9},{9,10},{10,11},{11... | collective-permute-start | bytes 4423688 | tf_op jit(solution)/shard_map/ppermute | solution.py:293
  13.8 23.6 %collective-permute-start.3 = (bf16[2,2,1440,128]{3,2,1,0:T(8,128)(2,1)S(1)}, bf16[2,2,1440,128]{3,2,1,0:T(8,128)(2,1)}, u32[]{:S(2)}, u32[]{:S(2)}) collective-permute-start(bf16[2,2,1440,128]{3,2,1,0:T(8,128)(2,1)S(1)} %get-tuple-element.29), channel_id=1, source_target_pairs={{1,0},{2,1},{3,2},{4,3},{5,4},{6,5},{7,6},{9,8},{10,9},{11,10},{12... | collective-permute-start | bytes 4423688 | tf_op jit(solution)/shard_map/ppermute | solution.py:294
  15.1 2.2 copy-start
  54.3 23.6 %copy-start.4 = (f32[69,2,1440]{2,1,0:T(2,128)S(1)}, f32[69,2,1440]{2,1,0:T(2,128)}, u32[]{:S(2)}) copy-start(f32[69,2,1440]{2,1,0:T(2,128)} %param.9) | copy-start | bytes 2384644
  73.5 4.6 %copy-start.6 = (f32[69]{0:T(128)S(1)}, f32[69]{0:T(128)}, u32[]{:S(2)}) copy-start(f32[69]{0:T(128)} %param.11) | copy-start | bytes 832
  73.5 4.6 %copy-start.7 = (f32[69]{0:T(128)S(1)}, f32[69]{0:T(128)}, u32[]{:S(2)}) copy-start(f32[69]{0:T(128)} %param.10) | copy-start | bytes 832
  73.5 18.6 %all-to-all-start = ((bf16[4,2,144,384]{3,2,1,0:T(8,128)(2,1)}), bf16[4,2,144,384]{3,2,1,0:T(8,128)(2,1)}, u32[]{:S(2)}, u32[]{:S(2)}) async-start(bf16[4,2,144,384]{3,2,1,0:T(8,128)(2,1)} %get-tuple-element.15), calls=%async_computation | async-start | bytes 1769472 | tf_op jit(solution)/shard_map/all_to_all | solution.py:382
  129.3 68.5 %copy-start.3 = (bf16[4,2,144,384]{3,2,1,0:T(8,128)(2,1)}, bf16[4,2,144,384]{3,2,1,0:T(8,128)(2,1)S(1)}, u32[]{:S(2)}) copy-start(bf16[4,2,144,384]{3,2,1,0:T(8,128)(2,1)S(1)} %all_to_all.35.own) | copy-start | bytes 2654212
  129.3 38.7 %all-to-all-start.2 = ((bf16[4,2,144,384]{3,2,1,0:T(8,128)(2,1)}), bf16[4,2,144,384]{3,2,1,0:T(8,128)(2,1)S(1)}, u32[]{:S(2)}, u32[]{:S(2)}) async-start(bf16[4,2,144,384]{3,2,1,0:T(8,128)(2,1)} %get-tuple-element.19), calls=%async_computation.2 | async-start | bytes 1769472 | tf_op jit(solution)/shard_map/all_to_all | solution.py:456
  132.8 65.0 %collective-permute-start.6 = (bf16[4,2,144,384]{3,2,1,0:T(8,128)(2,1)S(1)}, bf16[4,2,144,384]{3,2,1,0:T(8,128)(2,1)}, u32[]{:S(2)}, u32[]{:S(2)}) collective-permute-start(bf16[4,2,144,384]{3,2,1,0:T(8,128)(2,1)S(1)} %all_to_all.35.own), channel_id=1, source_target_pairs={{0,1},{1,2},{2,3},{3,4},{4,5},{5,6},{6,7},{8,9},{9,10},{10,11},{11... | collective-permute-start | bytes 2654216 | tf_op jit(solution)/shard_map/ppermute | solution.py:293
  166.6 31.2 %collective-permute-start.7 = (bf16[4,2,144,384]{3,2,1,0:T(8,128)(2,1)S(1)}, bf16[4,2,144,384]{3,2,1,0:T(8,128)(2,1)}, u32[]{:S(2)}, u32[]{:S(2)}) collective-permute-start(bf16[4,2,144,384]{3,2,1,0:T(8,128)(2,1)S(1)} %all_to_all.35.own), channel_id=1, source_target_pairs={{1,0},{2,1},{3,2},{4,3},{5,4},{6,5},{7,6},{9,8},{10,9},{11,10},{12... | collective-permute-start | bytes 2654216 | tf_op jit(solution)/shard_map/ppermute | solution.py:294
  167.9 44.4 %copy-start.2 = (bf16[4,2,144,384]{3,2,1,0:T(8,128)(2,1)}, bf16[4,2,144,384]{3,2,1,0:T(8,128)(2,1)S(1)}, u32[]{:S(2)}) copy-start(bf16[4,2,144,384]{3,2,1,0:T(8,128)(2,1)S(1)} %all-to-all-done.2.own) | copy-start | bytes 2654212
  168.0 44.4 %collective-permute-start.4 = (bf16[4,2,144,384]{3,2,1,0:T(8,128)(2,1)S(1)}, bf16[4,2,144,384]{3,2,1,0:T(8,128)(2,1)}, u32[]{:S(2)}, u32[]{:S(2)}) collective-permute-start(bf16[4,2,144,384]{3,2,1,0:T(8,128)(2,1)S(1)} %all-to-all-done.2.own), channel_id=1, source_target_pairs={{0,1},{1,2},{2,3},{3,4},{4,5},{5,6},{6,7},{8,9},{9,10},{10,11},{11... | collective-permute-start | bytes 2654216 | tf_op jit(solution)/shard_map/ppermute | solution.py:293
  195.1 20.5 %collective-permute-start.5 = (bf16[4,2,144,384]{3,2,1,0:T(8,128)(2,1)S(1)}, bf16[4,2,144,384]{3,2,1,0:T(8,128)(2,1)}, u32[]{:S(2)}, u32[]{:S(2)}) collective-permute-start(bf16[4,2,144,384]{3,2,1,0:T(8,128)(2,1)S(1)} %all-to-all-done.2.own), channel_id=1, source_target_pairs={{1,0},{2,1},{3,2},{4,3},{5,4},{6,5},{7,6},{9,8},{10,9},{11,10},{12... | collective-permute-start | bytes 2654216 | tf_op jit(solution)/shard_map/ppermute | solution.py:294
  215.6 14.7 %copy-start.1 = (f32[1800,128]{1,0:T(8,128)S(1)}, f32[1800,128]{1,0:T(8,128)}, u32[]{:S(2)}) copy-start(f32[1800,128]{1,0:T(8,128)} %get-tuple-element.25) | copy-start | bytes 2764804
  265.0 18.6 %all-to-all-start.5 = ((bf16[32,64,128]{2,1,0:T(8,128)(2,1)}), bf16[32,64,128]{2,1,0:T(8,128)(2,1)S(1)}, u32[]{:S(2)}, u32[]{:S(2)}) async-start(bf16[32,64,128]{2,1,0:T(8,128)(2,1)} %broadcast_in_dim.28), calls=%async_computation.5 | async-start | bytes 1048576 | tf_op jit(solution)/shard_map/all_to_all | solution.py:306

commit v3 on v2

--- a/solution.py
+++ b/solution.py
@@ -13,10 +13,11 @@
 F32 = jnp.float32
 LANES = 128
 EDGE = 16
-VMEM_LIMIT = 60 * 1024 * 1024
+MIB = 1024 * 1024
+FWD_MIB, PAIR_MIB, BACK_MIB, LAST_MIB = 60, 44, 44, 56
 TILE = 480
-AHEAD = 2
-BACK = 2
+AHEAD = (2, 1)
+BEHIND = 2
 
 
 def tile_of(count, step, most):
@@ -44,17 +45,22 @@
 
 
 def forward_kernel(dims, flags, own, top, bot, w_inner, w_head, *refs):
-    rows, lon, lon_pad, ch, qp, pieces, piece = dims
+    rows, lon, lon_pad, ch, qp, pieces, piece, relay = dims
+    relayed = refs[0] if relay else None
     hidden_out, slope_out, field_out, xs, hs, fs = refs[-6:]
     tile = tile_of(lon, 16, TILE)
     half = math.sqrt(2.0 / math.pi)
     for j in range(rows + 4):
         if j < 2:
             row = top[0, j]
+            if relayed is not None:
+                row = jnp.where(flags[2] != 0, relayed[0, j], row)
         elif j < rows + 2:
             row = own[0, j - 2]
         else:
             row = bot[0, j - rows - 2]
+            if relayed is not None:
+                row = jnp.where(flags[3] != 0, relayed[0, j - rows - 2], row)
         xs[EDGE : EDGE + lon, j * ch : (j + 1) * ch] = row
     wrap_edges(xs, lon)
     top_ok = flags[0].astype(F32)
@@ -279,19 +285,19 @@
     return jnp.stack(cols, axis=3).reshape(3, 4 * width, 2 * ch)
 
 
-def groups_of(count, groups):
-    out, first = [], 0
+def groups_of(first, count, groups):
+    out, end = [], first + count
     for g in range(min(groups, count)):
-        size = -(-(count - first) // (min(groups, count) - g))
+        size = -(-(end - first) // (min(groups, count) - g))
         out.append((first, size))
         first += size
     return out
 
 
-def neighbours(tail, head, axis):
-    count = lax.axis_size(axis)
-    before = lax.ppermute(tail, axis, [(i, i + 1) for i in range(count - 1)])
-    after = lax.ppermute(head, axis, [(i + 1, i) for i in range(count - 1)])
+def neighbours(tail, head, axis, skip=None):
+    edges = [(i, i + 1) for i in range(lax.axis_size(axis) - 1) if i + 1 != skip]
+    before = lax.ppermute(tail, axis, edges)
+    after = lax.ppermute(head, axis, [(j, i) for i, j in edges])
     return before, after
 
 
@@ -323,14 +329,14 @@
     span = -(-(5 * vp - low) // 16) * 16
 
     at = lax.axis_index("lat")
-    flags = jnp.stack([at > 0, at < lax.axis_size("lat") - 1]).astype(jnp.int32)
+    count = lax.axis_size("lat")
+    middle = count // 2
+    flags = jnp.stack([at > 0, at < count - 1, at == middle, at == middle - 1]).astype(jnp.int32)
 
     w_inner = forward_weights(conv_inner, ch)
     w_head = jnp.pad(forward_weights(conv_head, vp), ((0, 0), (0, 0), (0, 256 - 2 * vp)))
-    w_back = backward_weights(conv_head, vp).reshape(12 * vp, 2 * ch)
-    w_grad = backward_weights(conv_inner, ch)
-
-    params = functools.partial(pltpu.CompilerParams, vmem_limit_bytes=VMEM_LIMIT)
+
+    params = lambda mib: pltpu.CompilerParams(vmem_limit_bytes=mib * MIB)
     whole = lambda shape: pl.BlockSpec(shape, lambda m: (0,) * len(shape))
     member = lambda shape, base=0: pl.BlockSpec((1,) + shape, lambda m: (base + m,) + (0,) * len(shape))
     spread = lambda n: pl.BlockSpec((pieces, 1, n, piece), lambda m: (0, m, 0, 0))
@@ -340,13 +346,14 @@
         jax.ShapeDtypeStruct((per, rows, lon_pad, ch), BF16),
         jax.ShapeDtypeStruct((per, rows + 2, lon_pad, ch), BF16),
     ]
-    ahead, behind = groups_of(per, AHEAD), groups_of(per, BACK)
-
-    def forward(first, count, kept):
-        mine = features[first : first + count]
-        top, bot = neighbours(mine[:, rows - 2 :], mine[:, :2], "lat")
+    groups, behind = groups_of(0, per, len(AHEAD)), groups_of(0, per, BEHIND)
+    calls = [groups_of(*group, parts) for group, parts in zip(groups, AHEAD)]
+
+    def forward(first, count, group, top, bot, relayed, kept):
+        field_shape = jax.ShapeDtypeStruct((pieces, group[1], qp, piece), BF16)
+        dims = (rows, lon, lon_pad, ch, qp, pieces, piece)
         return pl.pallas_call(
-            functools.partial(forward_kernel, (rows, lon, lon_pad, ch, qp, pieces, piece)),
+            functools.partial(forward_kernel, dims + (len(relayed),)),
             grid=(count,),
             in_specs=[
                 pl.BlockSpec(memory_space=pltpu.SMEM),
@@ -356,36 +363,65 @@
                 whole(w_inner.shape),
                 whole(w_head.shape),
             ]
+            + [member((2, lon, ch), first - groups[-1][0]) for _ in relayed]
             + [pl.BlockSpec(memory_space=pl.ANY)] * len(kept),
             out_specs=[
                 member((rows, lon_pad, ch), first),
                 member((rows + 2, lon_pad, ch), first),
-                spread(qp),
+                pl.BlockSpec((pieces, 1, qp, piece), lambda m: (0, first - group[0] + m, 0, 0)),
             ],
-            out_shape=kept_shapes + [jax.ShapeDtypeStruct((pieces, count, qp, piece), BF16)],
-            input_output_aliases={6 + k: k for k in range(len(kept))},
+            out_shape=kept_shapes + [field_shape],
+            input_output_aliases={6 + len(relayed) + k: k for k in range(len(kept))},
             scratch_shapes=[
                 pltpu.VMEM((lon + 2 * EDGE, (rows + 4) * ch), BF16),
                 pltpu.VMEM((lon + 2 * EDGE, (rows + 2) * ch), BF16),
                 pltpu.VMEM((rows // 2, lon_pad, 256), F32),
             ],
-            compiler_params=params(),
+            compiler_params=params(FWD_MIB),
             cost_estimate=pl.CostEstimate(
                 flops=3 * macs * count, bytes_accessed=(6 << 20) * count, transcendentals=0
             ),
             name="forward",
-        )(flags, features, top, bot, w_inner, w_head, *kept)
-
-    kept, traded = [], []
-    for first, count in ahead:
-        *kept, field = forward(first, count, kept)
-        traded.append(lax.all_to_all(field, "mem", 0, 0, tiled=True))
-
+        )(flags, features, top, bot, w_inner, w_head, *relayed, *kept)
+
+    start, size = groups[-1]
+    mine = features[start : start + size]
+    edge = mine
+    if rows > 2:
+        edge = jnp.where(at == middle, mine[:, :2], mine[:, rows - 2 :])
+    half = lax.ppermute(edge, "lat", [(middle - 1, count - 1), (middle, 0)])
+    relayed = lax.ppermute(half, "lat", [(count - 1, middle), (0, middle - 1)])
+    halos = []
+    for first, number in sum(calls, []):
+        mine = features[first : first + number]
+        skip = middle if first >= start else None
+        halos.append(neighbours(mine[:, rows - 2 :], mine[:, :2], "lat", skip))
+
+    kept, traded, called = [], [], 0
+    for group, parts in zip(groups, calls):
+        field = []
+        for first, number in parts:
+            *kept, field = forward(
+                first,
+                number,
+                group,
+                *halos[called],
+                [relayed] if first >= start else [],
+                [*kept[:2], *field],
+            )
+            called, field = called + 1, [field]
+        traded.append(lax.all_to_all(field[0], "mem", 0, 0, tiled=True))
+
+    conv_inner, conv_head, truth, kernel_width, var_weight, _ = lax.optimization_barrier(
+        (conv_inner, conv_head, truth, kernel_width, var_weight, field[0])
+    )
+    w_back = backward_weights(conv_head, vp).reshape(12 * vp, 2 * ch)
+    w_grad = backward_weights(conv_inner, ch)
     truth_rows = jnp.moveaxis(truth, 1, 0)
     truth_rows = jnp.pad(truth_rows, ((0, 0), (0, vp - variables), (0, 0))).reshape(qp, lon)
-    middle = jnp.zeros((qp, lon_pad - lon - 2 * EDGE), F32)
+    blank = jnp.zeros((qp, lon_pad - lon - 2 * EDGE), F32)
     truth_rows = jnp.concatenate(
-        [truth_rows, truth_rows[:, :EDGE], middle, truth_rows[:, lon - EDGE :]], axis=1
+        [truth_rows, truth_rows[:, :EDGE], blank, truth_rows[:, lon - EDGE :]], axis=1
     )
     truth_piece = lax.dynamic_slice_in_dim(truth_rows, lax.axis_index("mem") * piece, piece, 1)
     inverse = 1.0 / (kernel_width * kernel_width)
@@ -398,16 +434,16 @@
     row_block = lambda width: pl.BlockSpec((sub, width), lambda i: (i, 0))
     field_block = lambda count: pl.BlockSpec((pieces, count, sub, piece), lambda i: (0, 0, i, 0))
     gradient = pl.pallas_call(
-        functools.partial(pair_kernel, (members, len(ahead), len(behind), sub, piece)),
+        functools.partial(pair_kernel, (members, len(groups), len(behind), sub, piece)),
         grid=(qp // sub,),
         in_specs=[row_block(piece), row_block(LANES), row_block(LANES)]
-        + [field_block(count) for _, count in ahead],
+        + [field_block(count) for _, count in groups],
         out_specs=[field_block(count) for _, count in behind],
         out_shape=[
             jax.ShapeDtypeStruct((pieces, count, qp, piece), BF16) for _, count in behind
         ],
         scratch_shapes=[pltpu.VMEM((members, sub, piece), F32)] * 2,
-        compiler_params=params(),
+        compiler_params=params(PAIR_MIB),
         cost_estimate=pl.CostEstimate(
             flops=4 * members * members * qp * piece,
             bytes_accessed=4 * members * qp * piece,
@@ -444,7 +480,7 @@
                 pltpu.VMEM((6 * ch, 4 * ch), F32),
                 pltpu.VMEM((3 * span, 2 * ch), F32),
             ],
-            compiler_params=params(),
+            compiler_params=params(BACK_MIB),
             cost_estimate=pl.CostEstimate(
                 flops=4 * macs * count, bytes_accessed=(6 << 20) * count, transcendentals=0
             ),
@@ -464,7 +500,7 @@
         out_specs=member((rows, lon, ch)),
         out_shape=jax.ShapeDtypeStruct(features.shape, BF16),
         scratch_shapes=[pltpu.VMEM((lon + 2 * EDGE, (rows + 2) * ch), BF16)],
-        compiler_params=params(),
+        compiler_params=params(LAST_MIB),
         cost_estimate=pl.CostEstimate(
             flops=macs * per, bytes_accessed=(4 << 20) * per, transcendentals=0
         ),

time: 286 us -> 253 us (0.88)
  starting transfers between devices: 85.7 us -> 58.3 us
  blocking collectives: 76.5 us -> 52.2 us
  waiting for transfers between devices: 18.8 us -> 34.3 us
  local copies, waits for them, and re-layouts: 14.9 us -> 20.6 us
    ppermute x8 -> x12, starting transfers between devices: 74.8 us -> 40 us  [the longest x5 17.6 us: neighbours(): before = lax.ppermute(tail, axis, edges)]
    all_to_all x1 -> x0, blocking collectives: 19.2 us -> none  [shards(): traded.append(lax.all_to_all(field, 'mem', 0, 0, tiled=True))]
    all_to_all x1, waiting for transfers between devices: 0.01 us -> 15.5 us  [shards(): owned.append(lax.all_to_all(g, 'mem', 0, 0, tiled=True))]
    all_to_all x1 -> x2, starting transfers between devices: 4.34 us -> 10.9 us  [shards(): traded.append(lax.all_to_all(field[0], 'mem', 0, 0, tiled=True))]
    unnamed x18 -> x32, local copies, waits for them, and re-layouts: 1.04 us -> 4.21 us
    all_to_all x1 -> x2, waiting for transfers between devices: 12.7 us -> 14.6 us  [shards(): traded.append(lax.all_to_all(field[0], 'mem', 0, 0, tiled=True))]
    pallas_call x3 -> x4, Pallas kernels: 44.7 us -> 45.5 us  [the longest x3 36.2 us: forward(): pl.pallas_call(functools.partial(forward_kernel, dims + (len(relayed),)),...]
  transfers between devices with their start and end apart: 11 -> 16, of which waited for: 3 -> 5; matrix products, arithmetic and copies ran while one was open for 4% -> 5% of each run, Pallas kernels for 15% -> 24%
where the time goes in v3:
time: 253 us
  Pallas kernels  83.1 us (33%)
  starting transfers between devices  58.3 us (23%)
  blocking collectives  52.2 us (21%)
  waiting for transfers between devices  34.3 us (14%)
  local copies, waits for them, and re-layouts  20.6 us (8%)
  other arithmetic  2.81 us (1%)
    pallas_call x3, Pallas kernels, forward(): pl.pallas_call(functools.partial(forward_kernel, dims + (len(relayed),)),...  36.2 us
    all_to_all x1, blocking collectives, reduce_all(): got = lax.all_to_all(padded, axes, 0, 0, tiled=True)  29.9 us
    pallas_call x2, Pallas kernels, backward(): pl.pallas_call(functools.partial(backward_kernel, (rows, lon, lon_pad, ch...  27.2 us
    all_to_all x1, blocking collectives, shards(): owned.append(lax.all_to_all(g, 'mem', 0, 0, tiled=True))  22.4 us
    ppermute x5, starting transfers between devices, neighbours(): before = lax.ppermute(tail, axis, edges)  17.6 us
    all_to_all x1, waiting for transfers between devices, shards(): owned.append(lax.all_to_all(g, 'mem', 0, 0, tiled=True))  15.5 us
    ppermute x1, starting transfers between devices, shards(): relayed = lax.ppermute(half, 'lat', [(count - 1, middle), (0, middle - 1)])  14.7 us
    all_to_all x2, waiting for transfers between devices, shards(): traded.append(lax.all_to_all(field[0], 'mem', 0, 0, tiled=True))  14.6 us
  transfers between devices with their start and end apart: 16, of which 5 were waited for; matrix products, arithmetic and copies ran while one was open for 5% of the time, Pallas kernels for 24%

profile of v3, /device:TPU:0, one launch (start us, length us, event | category | flops | bytes accessed | tf_op | source)
XLA Modules:
  0.0 252.5 jit_solution(11883978522307125173)
XLA Ops:
  0.7 2.7 %slice.28 = bf16[2,2,1440,128]{3,2,1,0:T(8,128)(2,1)} slice(bf16[4,2,1440,128]{3,2,1,0:T(8,128)(2,1)} %feats.3), slice={[2:4], [0:2], [0:1440], [0:128]} | slice | bytes 2949120 | tf_op jit(solution)/shard_map/slice | solution.py:396
  3.4 1.3 collective-permute-start.2
  5.7 2.9 %collective-permute-start.6 = (bf16[1,2,1440,128]{3,2,1,0:T(8,128)(2,1)S(1)}, bf16[1,2,1440,128]{3,2,1,0:T(8,128)(2,1)S(1)}, u32[]{:S(2)}, u32[]{:S(2)}) collective-permute-start(bf16[1,2,1440,128]{3,2,1,0:T(8,128)(2,1)S(1)} %get-tuple-element.45), channel_id=1, source_target_pairs={{0,1},{1,2},{2,3},{3,4},{4,5},{5,6},{6,7},{8,9},{9,10},{10,11},{11... | collective-permute-start | bytes 2211848 | tf_op jit(solution)/shard_map/ppermute | solution.py:299
  8.6 1.3 collective-permute-start.7
  9.9 5.1 %collective-permute-start.4 = (bf16[1,2,1440,128]{3,2,1,0:T(8,128)(2,1)}, bf16[1,2,1440,128]{3,2,1,0:T(8,128)(2,1)S(1)}, u32[]{:S(2)}, u32[]{:S(2)}) collective-permute-start(bf16[1,2,1440,128]{3,2,1,0:T(8,128)(2,1)} %get-tuple-element.46), channel_id=1, source_target_pairs={{0,1},{1,2},{2,3},{3,4},{4,5},{5,6},{6,7},{8,9},{9,10},{10,11},{11... | collective-permute-start | bytes 2211848 | tf_op jit(solution)/shard_map/ppermute | solution.py:299
  15.0 1.3 collective-permute-start.5
  16.7 6.0 %collective-permute-start = (bf16[2,2,1440,128]{3,2,1,0:T(8,128)(2,1)}, bf16[2,2,1440,128]{3,2,1,0:T(8,128)(2,1)}, u32[]{:S(2)}, u32[]{:S(2)}) collective-permute-start(bf16[2,2,1440,128]{3,2,1,0:T(8,128)(2,1)} %slice.28), channel_id=1, source_target_pairs={{0,1},{1,2},{2,3},{4,5},{5,6},{6,7},{8,9},{9,10},{10,11},{12,13},{... | collective-permute-start | bytes 4423688 | tf_op jit(solution)/shard_map/ppermute | solution.py:299
  22.7 1.3 collective-permute-start.1
  23.9 1.4 collective-permute-done.2
  25.3 14.7 %collective-permute-start.3 = (bf16[2,2,1440,128]{3,2,1,0:T(8,128)(2,1)}, bf16[2,2,1440,128]{3,2,1,0:T(8,128)(2,1)}, u32[]{:S(2)}, u32[]{:S(2)}) collective-permute-start(bf16[2,2,1440,128]{3,2,1,0:T(8,128)(2,1)} %collective-permute-done.2), channel_id=1, source_target_pairs={{7,4},{0,3},{15,12},{8,11},{23,20},{16,19},{31,28},{24,27}} | collective-permute-start | bytes 4423688 | tf_op jit(solution)/shard_map/ppermute | solution.py:393
  43.0 1.4 reshape.36.w_inner
  45.0 9.4 %forward.3 = (bf16[4,2,1536,128]{3,2,1,0:T(8,128)(2,1)}, bf16[4,4,1536,128]{3,2,1,0:T(8,128)(2,1)}, bf16[4,2,144,384]{3,2,1,0:T(8,128)(2,1)}) custom-call(s32[4]{0:T(128)} %add_convert_fusion.1.flags, bf16[4,2,1440,128]{3,2,1,0:T(8,128)(2,1)} %feats.3, bf16[1,2,1440,128]{3,2,1,0:T(8,128)(2,1)} %copy-done.13, bf16[1,2,1440,128]{3,2,1,0:T(8,128)(2,1)} %copy-done.14, ...), custom_call_target="tpu_custom_call" | custom-call | flops 3397386240 | bytes 6291456 | tf_op jit(solution)/shard_map/forward/pallas_call | solution.py:355
  55.2 9.4 %forward.4 = (bf16[4,2,1536,128]{3,2,1,0:T(8,128)(2,1)}, bf16[4,4,1536,128]{3,2,1,0:T(8,128)(2,1)}, bf16[4,2,144,384]{3,2,1,0:T(8,128)(2,1)}) custom-call(s32[4]{0:T(128)} %add_convert_fusion.1.flags, bf16[4,2,1440,128]{3,2,1,0:T(8,128)(2,1)} %feats.3, ...), custom_call_target="tpu_custom_call", output_to_operand_aliasing={{0}: (6, {}), {1}: (7, {}), {2}: (8, {})} | custom-call | flops 3397386240 | bytes 6291456 | tf_op jit(solution)/shard_map/forward/pallas_call | solution.py:355
  64.7 5.9 %all-to-all-start = ((bf16[4,2,144,384]{3,2,1,0:T(8,128)(2,1)}), bf16[4,2,144,384]{3,2,1,0:T(8,128)(2,1)S(1)}, u32[]{:S(2)}, u32[]{:S(2)}) async-start(bf16[4,2,144,384]{3,2,1,0:T(8,128)(2,1)} %get-tuple-element.32), calls=%async_computation | async-start | bytes 1769472 | tf_op jit(solution)/shard_map/all_to_all | solution.py:413
  70.6 17.4 %forward.5 = (bf16[4,2,1536,128]{3,2,1,0:T(8,128)(2,1)}, bf16[4,4,1536,128]{3,2,1,0:T(8,128)(2,1)}, bf16[4,2,144,384]{3,2,1,0:T(8,128)(2,1)}) custom-call(s32[4]{0:T(128)} %add_convert_fusion.1.flags, bf16[4,2,1440,128]{3,2,1,0:T(8,128)(2,1)} %feats.3, ...), custom_call_target="tpu_custom_call", output_to_operand_aliasing={{0}: (7, {}), {1}: (8, {})} | custom-call | flops 6794772480 | bytes 12582912 | tf_op jit(solution)/shard_map/forward/pallas_call | solution.py:355
  88.1 5.0 %all-to-all-start.1 = ((bf16[4,2,144,384]{3,2,1,0:T(8,128)(2,1)}), bf16[4,2,144,384]{3,2,1,0:T(8,128)(2,1)S(1)}, u32[]{:S(2)}, u32[]{:S(2)}) async-start(bf16[4,2,144,384]{3,2,1,0:T(8,128)(2,1)} %get-tuple-element.28), calls=%async_computation.1 | async-start | bytes 1769472 | tf_op jit(solution)/shard_map/all_to_all | solution.py:413
  96.2 14.5 %all-to-all-done.1.refs_1_ = bf16[4,2,144,384]{3,2,1,0:T(8,128)(2,1)S(1)} async-done(((bf16[4,2,144,384]{3,2,1,0:T(8,128)(2,1)}), bf16[4,2,144,384]{3,2,1,0:T(8,128)(2,1)S(1)}, u32[]{:S(2)}, u32[]{:S(2)}) %all-to-all-start.1) | async-done | bytes 884768 | tf_op jit(solution)/shard_map/all_to_all | solution.py:413
  110.8 9.3 %pairs.1 = (bf16[4,2,144,384]{3,2,1,0:T(8,128)(2,1)S(1)}, bf16[4,2,144,384]{3,2,1,0:T(8,128)(2,1)S(1)}) custom-call(f32[144,384]{1,0:T(8,128)S(1)} %constant_dynamic-slice_fusion.truth, f32[144,128]{1,0:T(8,128)S(1)} %broadcast_in_dim.25.rate, f32[144,128]{1,0:T(8,128)S(1)} %broadcast_in_dim.27.scale, bf16[4,2,144,384]{3,2,1,0:T(8,128)(2,1)S(1)} %all-to-all-done.refs_0_, ...), custom_call_target="tpu_custom_call" | custom-call | flops 56623104 | bytes 3538944 | tf_op jit(solution)/shard_map/pairs/pallas_call | solution.py:436
  120.1 22.4 %all_to_all.34.own = bf16[4,2,144,384]{3,2,1,0:T(8,128)(2,1)} all-to-all(bf16[4,2,144,384]{3,2,1,0:T(8,128)(2,1)S(1)} %get-tuple-element.37), channel_id=1, replica_groups=mesh['mem'=4,'lat'=8] {'mem'}, dimensions={0} | all-to-all | bytes 1769472 | tf_op jit(solution)/shard_map/all_to_all | solution.py:492
  142.5 4.5 %all-to-all-start.2 = ((bf16[4,2,144,384]{3,2,1,0:T(8,128)(2,1)}), bf16[4,2,144,384]{3,2,1,0:T(8,128)(2,1)}, u32[]{:S(2)}, u32[]{:S(2)}) async-start(bf16[4,2,144,384]{3,2,1,0:T(8,128)(2,1)} %copy-done.4), calls=%async_computation.2 | async-start | bytes 1769472 | tf_op jit(solution)/shard_map/all_to_all | solution.py:492
  147.0 2.2 collective-permute-start.10
  152.2 15.5 %all-to-all-done.2.own = bf16[4,2,144,384]{3,2,1,0:T(8,128)(2,1)} async-done(((bf16[4,2,144,384]{3,2,1,0:T(8,128)(2,1)}), bf16[4,2,144,384]{3,2,1,0:T(8,128)(2,1)}, u32[]{:S(2)}, u32[]{:S(2)}) %all-to-all-start.2) | async-done | bytes 884768 | tf_op jit(solution)/shard_map/all_to_all | solution.py:492
  167.7 1.3 collective-permute-start.8
  169.1 1.3 collective-permute-start.9
  170.9 1.9 copy-done.2
  173.9 13.7 %backward.2 = (bf16[4,4,1536,128]{3,2,1,0:T(8,128)(2,1)}, f32[1800,128]{1,0:T(8,128)S(1)}) custom-call(bf16[4,2,144,384]{3,2,1,0:T(8,128)(2,1)S(1)} %copy-done.3, bf16[4,2,144,384]{3,2,1,0:T(8,128)(2,1)} %collective-permute-done.10.top, bf16[4,2,144,384]{3,2,1,0:T(8,128)(2,1)} %collective-permute-done.11.bot, bf16[4,2,1536,128]{3,2,1,0:T(8,128)(2,1)S(1)} %copy-done.2, ...), custom_call_target="tpu_custom_call" | custom-call | flops 9059696640 | bytes 12582912 | tf_op jit(solution)/shard_map/backward/pallas_call | solution.py:459
  187.6 13.6 %backward.3 = (bf16[4,4,1536,128]{3,2,1,0:T(8,128)(2,1)}, f32[1800,128]{1,0:T(8,128)S(1)}) custom-call(bf16[4,2,144,384]{3,2,1,0:T(8,128)(2,1)} %all-to-all-done.2.own, bf16[4,2,144,384]{3,2,1,0:T(8,128)(2,1)S(1)} %collective-permute-done.8.top, bf16[4,2,144,384]{3,2,1,0:T(8,128)(2,1)S(1)} %collective-permute-done.9.bot, ...), custom_call_target="tpu_custom_call", output_to_operand_aliasing={{0}: (7, {})} | custom-call | flops 9059696640 | bytes 12582912 | tf_op jit(solution)/shard_map/backward/pallas_call | solution.py:459
  201.3 29.9 %all_to_all.35 = bf16[32,64,128]{2,1,0:T(8,128)(2,1)S(1)} all-to-all(bf16[32,64,128]{2,1,0:T(8,128)(2,1)S(1)} %bitcast.53), channel_id=1, replica_groups=mesh['mem'=4,'lat'=8] {'mem','lat'}, dimensions={0} | all-to-all | bytes 1048576 | tf_op jit(solution)/shard_map/all_to_all | solution.py:309
  232.2 3.0 %all-to-all-start.5 = ((bf16[32,64,128]{2,1,0:T(8,128)(2,1)}), bf16[32,64,128]{2,1,0:T(8,128)(2,1)S(1)}, u32[]{:S(2)}, u32[]{:S(2)}) async-start(bf16[32,64,128]{2,1,0:T(8,128)(2,1)} %broadcast_in_dim.28), calls=%async_computation.5 | async-start | bytes 1048576 | tf_op jit(solution)/shard_map/all_to_all | solution.py:312
  236.1 1.4 reshape.39.w_grad
  237.5 10.5 %features.1 = bf16[4,2,1440,128]{3,2,1,0:T(8,128)(2,1)} custom-call(bf16[4,4,1536,128]{3,2,1,0:T(8,128)(2,1)} %get-tuple-element.39.back, bf16[3,512,256]{2,1,0:T(8,128)(2,1)} %reshape.39.w_grad), custom_call_target="tpu_custom_call" | custom-call | flops 4529848320 | bytes 16777216 | tf_op jit(solution)/shard_map/features/pallas_call | solution.py:496
  247.9 2.9 %all-to-all-done.5 = bf16[32,64,128]{2,1,0:T(8,128)(2,1)S(1)} async-done(((bf16[32,64,128]{2,1,0:T(8,128)(2,1)}), bf16[32,64,128]{2,1,0:T(8,128)(2,1)S(1)}, u32[]{:S(2)}, u32[]{:S(2)}) %all-to-all-start.5) | async-done | bytes 524320 | tf_op jit(solution)/shard_map/all_to_all | solution.py:312
  (87 shorter events, 17.4 us)
Async XLA Ops:
  0.6 4.1 %copy-start = (bf16[4,2,1440,128]{3,2,1,0:T(8,128)(2,1)S(1)}, bf16[4,2,1440,128]{3,2,1,0:T(8,128)(2,1)}, u32[]{:S(2)}) copy-start(bf16[4,2,1440,128]{3,2,1,0:T(8,128)(2,1)} %feats.3) | copy-start | bytes 8847364
  0.6 15.7 %copy-start.9 = (bf16[3,3,128,69]{2,3,1,0:T(8,128)(2,1)S(1)}, bf16[3,3,128,69]{2,3,1,0:T(8,128)(2,1)}, u32[]{:S(2)}) copy-start(bf16[3,3,128,69]{2,3,1,0:T(8,128)(2,1)} %param.8) | copy-start | bytes 476932
  0.7 15.7 %copy-start.5 = (bf16[3,3,128,128]{3,2,1,0:T(8,128)(2,1)S(1)}, bf16[3,3,128,128]{3,2,1,0:T(8,128)(2,1)}, u32[]{:S(2)}) copy-start(bf16[3,3,128,128]{3,2,1,0:T(8,128)(2,1)} %param.7) | copy-start | bytes 884740
  3.4 21.9 %collective-permute-start.2 = (bf16[2,2,1440,128]{3,2,1,0:T(8,128)(2,1)}, bf16[2,2,1440,128]{3,2,1,0:T(8,128)(2,1)}, u32[]{:S(2)}, u32[]{:S(2)}) collective-permute-start(bf16[2,2,1440,128]{3,2,1,0:T(8,128)(2,1)} %slice.28), channel_id=1, source_target_pairs={{3,7},{4,0},{11,15},{12,8},{19,23},{20,16},{27,31},{28,24}} | collective-permute-start | bytes 4423688 | tf_op jit(solution)/shard_map/ppermute | solution.py:392
  5.7 11.0 %collective-permute-start.6 = (bf16[1,2,1440,128]{3,2,1,0:T(8,128)(2,1)S(1)}, bf16[1,2,1440,128]{3,2,1,0:T(8,128)(2,1)S(1)}, u32[]{:S(2)}, u32[]{:S(2)}) collective-permute-start(bf16[1,2,1440,128]{3,2,1,0:T(8,128)(2,1)S(1)} %get-tuple-element.45), channel_id=1, source_target_pairs={{0,1},{1,2},{2,3},{3,4},{4,5},{5,6},{6,7},{8,9},{9,10},{10,11},{11... | collective-permute-start | bytes 2211848 | tf_op jit(solution)/shard_map/ppermute | solution.py:299
  8.6 14.1 %collective-permute-start.7 = (bf16[1,2,1440,128]{3,2,1,0:T(8,128)(2,1)S(1)}, bf16[1,2,1440,128]{3,2,1,0:T(8,128)(2,1)S(1)}, u32[]{:S(2)}, u32[]{:S(2)}) collective-permute-start(bf16[1,2,1440,128]{3,2,1,0:T(8,128)(2,1)S(1)} %get-tuple-element.45), channel_id=1, source_target_pairs={{1,0},{2,1},{3,2},{4,3},{5,4},{6,5},{7,6},{9,8},{10,9},{11,10},{12... | collective-permute-start | bytes 2211848 | tf_op jit(solution)/shard_map/ppermute | solution.py:300
  9.9 44.5 %collective-permute-start.4 = (bf16[1,2,1440,128]{3,2,1,0:T(8,128)(2,1)}, bf16[1,2,1440,128]{3,2,1,0:T(8,128)(2,1)S(1)}, u32[]{:S(2)}, u32[]{:S(2)}) collective-permute-start(bf16[1,2,1440,128]{3,2,1,0:T(8,128)(2,1)} %get-tuple-element.46), channel_id=1, source_target_pairs={{0,1},{1,2},{2,3},{3,4},{4,5},{5,6},{6,7},{8,9},{9,10},{10,11},{11... | collective-permute-start | bytes 2211848 | tf_op jit(solution)/shard_map/ppermute | solution.py:299
  15.0 39.4 %collective-permute-start.5 = (bf16[1,2,1440,128]{3,2,1,0:T(8,128)(2,1)}, bf16[1,2,1440,128]{3,2,1,0:T(8,128)(2,1)}, u32[]{:S(2)}, u32[]{:S(2)}) collective-permute-start(bf16[1,2,1440,128]{3,2,1,0:T(8,128)(2,1)} %get-tuple-element.46), channel_id=1, source_target_pairs={{1,0},{2,1},{3,2},{4,3},{5,4},{6,5},{7,6},{9,8},{10,9},{11,10},{12... | collective-permute-start | bytes 2211848 | tf_op jit(solution)/shard_map/ppermute | solution.py:300
  16.7 23.4 %copy-start.13 = (bf16[1,2,1440,128]{3,2,1,0:T(8,128)(2,1)}, bf16[1,2,1440,128]{3,2,1,0:T(8,128)(2,1)S(1)}, u32[]{:S(2)}) copy-start(bf16[1,2,1440,128]{3,2,1,0:T(8,128)(2,1)S(1)} %collective-permute-done.6.top) | copy-start | bytes 2211844
  16.7 53.9 %collective-permute-start = (bf16[2,2,1440,128]{3,2,1,0:T(8,128)(2,1)}, bf16[2,2,1440,128]{3,2,1,0:T(8,128)(2,1)}, u32[]{:S(2)}, u32[]{:S(2)}) collective-permute-start(bf16[2,2,1440,128]{3,2,1,0:T(8,128)(2,1)} %slice.28), channel_id=1, source_target_pairs={{0,1},{1,2},{2,3},{4,5},{5,6},{6,7},{8,9},{9,10},{10,11},{12,13},{... | collective-permute-start | bytes 4423688 | tf_op jit(solution)/shard_map/ppermute | solution.py:299
  22.7 17.4 %copy-start.14 = (bf16[1,2,1440,128]{3,2,1,0:T(8,128)(2,1)}, bf16[1,2,1440,128]{3,2,1,0:T(8,128)(2,1)S(1)}, u32[]{:S(2)}) copy-start(bf16[1,2,1440,128]{3,2,1,0:T(8,128)(2,1)S(1)} %collective-permute-done.7.bot) | copy-start | bytes 2211844
  22.7 47.9 %collective-permute-start.1 = (bf16[2,2,1440,128]{3,2,1,0:T(8,128)(2,1)}, bf16[2,2,1440,128]{3,2,1,0:T(8,128)(2,1)}, u32[]{:S(2)}, u32[]{:S(2)}) collective-permute-start(bf16[2,2,1440,128]{3,2,1,0:T(8,128)(2,1)} %slice.28), channel_id=1, source_target_pairs={{1,0},{2,1},{3,2},{5,4},{6,5},{7,6},{9,8},{10,9},{11,10},{13,12},{... | collective-permute-start | bytes 4423688 | tf_op jit(solution)/shard_map/ppermute | solution.py:300
  25.3 45.3 %collective-permute-start.3 = (bf16[2,2,1440,128]{3,2,1,0:T(8,128)(2,1)}, bf16[2,2,1440,128]{3,2,1,0:T(8,128)(2,1)}, u32[]{:S(2)}, u32[]{:S(2)}) collective-permute-start(bf16[2,2,1440,128]{3,2,1,0:T(8,128)(2,1)} %collective-permute-done.2), channel_id=1, source_target_pairs={{7,4},{0,3},{15,12},{8,11},{23,20},{16,19},{31,28},{24,27}} | collective-permute-start | bytes 4423688 | tf_op jit(solution)/shard_map/ppermute | solution.py:393
  54.4 0.9 copy-start.8
  64.7 23.4 %all-to-all-start = ((bf16[4,2,144,384]{3,2,1,0:T(8,128)(2,1)}), bf16[4,2,144,384]{3,2,1,0:T(8,128)(2,1)S(1)}, u32[]{:S(2)}, u32[]{:S(2)}) async-start(bf16[4,2,144,384]{3,2,1,0:T(8,128)(2,1)} %get-tuple-element.32), calls=%async_computation | async-start | bytes 1769472 | tf_op jit(solution)/shard_map/all_to_all | solution.py:413
  70.6 22.5 %copy-start.11 = (f32[69]{0:T(128)S(1)}, f32[69]{0:T(128)}, u32[]{:S(2)}) copy-start(f32[69]{0:T(128)} %param.11) | copy-start | bytes 832
  70.6 22.5 %copy-start.12 = (f32[69]{0:T(128)S(1)}, f32[69]{0:T(128)}, u32[]{:S(2)}) copy-start(f32[69]{0:T(128)} %param.10) | copy-start | bytes 832
  70.6 22.7 %copy-start.7 = (f32[69,2,1440]{2,1,0:T(2,128)S(1)}, f32[69,2,1440]{2,1,0:T(2,128)}, u32[]{:S(2)}) copy-start(f32[69,2,1440]{2,1,0:T(2,128)} %param.9) | copy-start | bytes 2384644
  88.1 22.5 %all-to-all-start.1 = ((bf16[4,2,144,384]{3,2,1,0:T(8,128)(2,1)}), bf16[4,2,144,384]{3,2,1,0:T(8,128)(2,1)S(1)}, u32[]{:S(2)}, u32[]{:S(2)}) async-start(bf16[4,2,144,384]{3,2,1,0:T(8,128)(2,1)} %get-tuple-element.28), calls=%async_computation.1 | async-start | bytes 1769472 | tf_op jit(solution)/shard_map/all_to_all | solution.py:413
  120.1 22.4 %copy-start.4 = (bf16[4,2,144,384]{3,2,1,0:T(8,128)(2,1)}, bf16[4,2,144,384]{3,2,1,0:T(8,128)(2,1)S(1)}, u32[]{:S(2)}) copy-start(bf16[4,2,144,384]{3,2,1,0:T(8,128)(2,1)S(1)} %get-tuple-element.33) | copy-start | bytes 2654212
  120.1 30.4 %copy-start.10 = (bf16[3,3,128,69]{2,3,1,0:T(8,128)(2,1)S(1)}, bf16[3,3,128,69]{2,3,1,0:T(8,128)(2,1)}, u32[]{:S(2)}) copy-start(bf16[3,3,128,69]{2,3,1,0:T(8,128)(2,1)} %param.8) | copy-start | bytes 476932
  142.5 28.4 %copy-start.1 = (bf16[4,2,1440,128]{3,2,1,0:T(8,128)(2,1)S(1)}, bf16[4,2,1440,128]{3,2,1,0:T(8,128)(2,1)}, u32[]{:S(2)}) copy-start(bf16[4,2,1440,128]{3,2,1,0:T(8,128)(2,1)} %feats.3) | copy-start | bytes 8847364
  142.5 25.2 %all-to-all-start.2 = ((bf16[4,2,144,384]{3,2,1,0:T(8,128)(2,1)}), bf16[4,2,144,384]{3,2,1,0:T(8,128)(2,1)}, u32[]{:S(2)}, u32[]{:S(2)}) async-start(bf16[4,2,144,384]{3,2,1,0:T(8,128)(2,1)} %copy-done.4), calls=%async_computation.2 | async-start | bytes 1769472 | tf_op jit(solution)/shard_map/all_to_all | solution.py:492
  147.0 23.9 %collective-permute-start.10 = (bf16[4,2,144,384]{3,2,1,0:T(8,128)(2,1)}, bf16[4,2,144,384]{3,2,1,0:T(8,128)(2,1)}, u32[]{:S(2)}, u32[]{:S(2)}) collective-permute-start(bf16[4,2,144,384]{3,2,1,0:T(8,128)(2,1)} %all_to_all.34.own), channel_id=1, source_target_pairs={{0,1},{1,2},{2,3},{3,4},{4,5},{5,6},{6,7},{8,9},{9,10},{10,11},{11... | collective-permute-start | bytes 2654216 | tf_op jit(solution)/shard_map/ppermute | solution.py:299
  149.2 21.6 %collective-permute-start.11 = (bf16[4,2,144,384]{3,2,1,0:T(8,128)(2,1)}, bf16[4,2,144,384]{3,2,1,0:T(8,128)(2,1)}, u32[]{:S(2)}, u32[]{:S(2)}) collective-permute-start(bf16[4,2,144,384]{3,2,1,0:T(8,128)(2,1)} %all_to_all.34.own), channel_id=1, source_target_pairs={{1,0},{2,1},{3,2},{4,3},{5,4},{6,5},{7,6},{9,8},{10,9},{11,10},{12... | collective-permute-start | bytes 2654216 | tf_op jit(solution)/shard_map/ppermute | solution.py:300
  167.7 19.9 %collective-permute-start.8 = (bf16[4,2,144,384]{3,2,1,0:T(8,128)(2,1)}, bf16[4,2,144,384]{3,2,1,0:T(8,128)(2,1)S(1)}, u32[]{:S(2)}, u32[]{:S(2)}) collective-permute-start(bf16[4,2,144,384]{3,2,1,0:T(8,128)(2,1)} %all-to-all-done.2.own), channel_id=1, source_target_pairs={{0,1},{1,2},{2,3},{3,4},{4,5},{5,6},{6,7},{8,9},{9,10},{10,11},{11... | collective-permute-start | bytes 2654216 | tf_op jit(solution)/shard_map/ppermute | solution.py:299
  169.1 18.5 %collective-permute-start.9 = (bf16[4,2,144,384]{3,2,1,0:T(8,128)(2,1)}, bf16[4,2,144,384]{3,2,1,0:T(8,128)(2,1)S(1)}, u32[]{:S(2)}, u32[]{:S(2)}) collective-permute-start(bf16[4,2,144,384]{3,2,1,0:T(8,128)(2,1)} %all-to-all-done.2.own), channel_id=1, source_target_pairs={{1,0},{2,1},{3,2},{4,3},{5,4},{6,5},{7,6},{9,8},{10,9},{11,10},{12... | collective-permute-start | bytes 2654216 | tf_op jit(solution)/shard_map/ppermute | solution.py:300
  170.9 1.9 copy-start.2
  172.8 1.2 copy-start.3
  201.1 34.1 %copy-start.6 = (bf16[3,3,128,128]{3,2,1,0:T(8,128)(2,1)S(1)}, bf16[3,3,128,128]{3,2,1,0:T(8,128)(2,1)}, u32[]{:S(2)}) copy-start(bf16[3,3,128,128]{3,2,1,0:T(8,128)(2,1)} %param.7) | copy-start | bytes 884740
  232.2 18.6 %all-to-all-start.5 = ((bf16[32,64,128]{2,1,0:T(8,128)(2,1)}), bf16[32,64,128]{2,1,0:T(8,128)(2,1)S(1)}, u32[]{:S(2)}, u32[]{:S(2)}) async-start(bf16[32,64,128]{2,1,0:T(8,128)(2,1)} %broadcast_in_dim.28), calls=%async_computation.5 | async-start | bytes 1048576 | tf_op jit(solution)/shard_map/all_to_all | solution.py:312
